TPU v7x, 32 devices: a whole 2x2x4 slice. The times are simulated.
32 devices in a mesh: ctx: 4 (over y, x), ep: 8 (over z, core).
Axes of the slice: x: 2, y: 2, z: 4, core: 2. Of those that a mesh axis runs over, the one named last changes fastest.
Arguments:
- block_input: bfloat16 [8, 512, 768], P('ep', 'ctx'), may hold values from -36 to 36
- out_grad: bfloat16 [8, 512, 768], P('ep', 'ctx'), may hold values from -6 to 6
- w_query: bfloat16 [768, 768], P('ep'), may hold values from -0.21875 to 0.21875
- w_key: bfloat16 [768, 768], P('ep'), may hold values from -0.21875 to 0.21875
- w_value: bfloat16 [768, 768], P('ep'), may hold values from -0.21875 to 0.21875
- w_output: bfloat16 [768, 768], P('ep'), may hold values from -0.875 to 0.875
- w_router: bfloat16 [768, 64], P('ep'), may hold values from -0.4375 to 0.4375
- attn_gain: bfloat16 [768], P('ep'), may hold values from 0.25 to 1.75
- moe_gain: bfloat16 [768], P('ep'), may hold values from 0.25 to 1.75
- bias_table: bfloat16 [32, 12], P('ep'), may hold values from -6 to 303
- rel_bucket: int32 [512], replicated, may hold values from 0 to 31
- expert_ids: int32 [8, 512, 2], P('ep', 'ctx'), may hold values from 0 to 63, all different within a row; in each aligned block of 128 rows (0 to 127, 128 to 255, ..., all dimensions but the last counted through in order) at most 6 rows name the same one
- expert_in: bfloat16 [64, 768, 3072], P('ep', None, 'ctx'), may hold values from -0.21875 to 0.21875
- expert_out: bfloat16 [64, 3072, 768], P('ep', 'ctx'), may hold values from -0.109375 to 0.109375
Outputs:
- block_output: float32 [8, 512, 768], P('ep', 'ctx')
- input_grad: float32 [8, 512, 768], P('ep', 'ctx')
- grad_query: float32 [768, 768], P('ep')
- grad_key: float32 [768, 768], P('ep')
- grad_value: float32 [768, 768], P('ep')
- grad_output: float32 [768, 768], P('ep')
- grad_router: float32 [768, 64], P('ep')
- grad_attn_gain: float32 [768], P('ep')
- grad_moe_gain: float32 [768], P('ep')
- grad_bias_table: float32 [32, 12], P('ep')
- grad_expert_in: float32 [64, 768, 3072], P('ep', None, 'ctx')
- grad_expert_out: float32 [64, 3072, 768], P('ep', 'ctx')
Inputs may be any that keep to these rules, and one draw needn't show every extreme that they name: `expert_ids`: each token names two different experts. Within each block of 128 positions of a sequence starting at a multiple of 128, no expert is named by more than 6 tokens, and some block has an expert named by exactly 6.
All inputs are finite; a program needn't handle non-finite values.
Results may differ from a plain program's by a relative error of at most 0.014.
Values may be sent and summed in bfloat16 or wider, within the bound.
No kernel may reach another device: no remote copies, remote signals or barrier semaphores. Data moves between devices by JAX's collectives and lax.ppermute only.
A program may use at most 448 MiB of HBM per device.

v0:
```python
import functools
import math

import jax
import jax.numpy as jnp
import numpy as np
from jax import lax
from jax.experimental import pallas as pl
from jax.experimental.pallas import tpu as pltpu
from jax.sharding import PartitionSpec as P


HD = 64
CAP = 6
TILE = 128
EXTRA = 128
HALVES = 2

EPS = 1e-06
SCALE = 0.125
INV_ROOT_TWO = 1.0 / math.sqrt(2.0)
INV_ROOT_TAU = 1.0 / math.sqrt(2.0 * math.pi)
NEG = -1e30

NN = (((1,), (0,)), ((), ()))
NT = (((1,), (1,)), ((), ()))
TN = (((0,), (0,)), ((), ()))


VMEM = pl.BlockSpec(memory_space=pltpu.VMEM)
SMEM = pl.BlockSpec(memory_space=pltpu.SMEM)


def f32(x):
    return x.astype(jnp.float32)


def b16(x):
    return x.astype(jnp.bfloat16)


def dot(a, b, dims=NN, precision=None):
    return lax.dot_general(a, b, dims, precision=precision, preferred_element_type=jnp.float32)


def iota(shape, axis):
    return lax.broadcasted_iota(jnp.int32, shape, axis)


def call(kernel, args, outs, scratch=(), flops=1e8, n_smem=1):
    size = sum(int(np.prod(a.shape)) * a.dtype.itemsize for a in args)
    size += sum(int(np.prod(s)) * jnp.dtype(d).itemsize for s, d in outs)
    return pl.pallas_call(
        kernel,
        out_shape=[jax.ShapeDtypeStruct(s, d) for s, d in outs],
        in_specs=[SMEM] * n_smem + [VMEM] * (len(args) - n_smem),
        out_specs=[VMEM] * len(outs),
        scratch_shapes=list(scratch),
        cost_estimate=pl.CostEstimate(flops=int(flops), bytes_accessed=size, transcendentals=0),
    )(*args)


def assemble(idx_ref, pieces, target, rows):
    if len(pieces) == 1:
        target[0 : pieces[0].shape[0], :] = pieces[0][...]
        return
    own = idx_ref[1]
    for order, piece in pieces:
        for n, off in enumerate(order):
            start = pl.multiple_of((own ^ off) * rows, rows)
            target[pl.ds(start, rows), :] = piece[n * rows : (n + 1) * rows, :]


def rms(x):
    inverse = lax.rsqrt(jnp.mean(x * x, axis=-1, keepdims=True) + EPS)
    return x * inverse, inverse


def table_select(buckets, width, rows, shards):
    per = buckets // shards
    b = iota((buckets, width), 0)
    shard = sum(((b >= per * s).astype(jnp.int32) for s in range(1, shards)), jnp.zeros_like(b))
    return iota((buckets, width), 1) == shard * rows + (b - shard * per)


def pack_weights(
    cfg, idx_ref, q_ref, k_ref, v_ref, o_ref, router_ref, one_ref, two_ref, table_ref, a_ref, b_ref, ext_ref
):
    R, CQ, D = cfg.rows, cfg.CQ, cfg.D
    width = cfg.NC * CQ
    shift = (cfg.NC - idx_ref[0]) * CQ
    for n, ref in enumerate((q_ref, k_ref, v_ref)):
        w = f32(ref[...])
        if width > D:
            w = jnp.concatenate([w, jnp.zeros((R, width - D), jnp.float32)], axis=1)
        a_ref[:, n * CQ : (n + 1) * CQ] = b16(pltpu.roll(w, shift, 1)[:, :CQ])
    ext_ref[...] = jnp.zeros_like(ext_ref)
    ext_ref[0 : table_ref.shape[0], 2 : 2 + cfg.H] = f32(table_ref[...])
    eye = (iota((R, R), 0) == iota((R, R), 1)).astype(jnp.float32)
    col_one = jnp.sum(eye * f32(one_ref[...]), axis=1, keepdims=True)
    col_two = jnp.sum(eye * f32(two_ref[...]), axis=1, keepdims=True)
    lane = iota((R, HD), 1)
    ext = ext_ref[:, :HD]
    ext = jnp.where(lane == 0, col_one, jnp.where(lane == 1, col_two, ext))
    a_ref[:, 3 * CQ :] = b16(ext)
    b_ref[:, :D] = o_ref[...]
    b_ref[:, D:] = b16(dot(b16(eye), router_ref[...], NT))


def place_blocks(cfg, idx_ref, pieces, target):
    for k, piece in enumerate(pieces):
        start = pl.multiple_of((idx_ref[0] ^ k) * cfg.B, cfg.B)
        target[pl.ds(start, cfg.B), :] = piece[...]


def attn_forward(cfg, idx_ref, bucket_ref, *refs):
    n_in = len(cfg.orders)
    pieces, refs = refs[:n_in], refs[n_in:]
    x_pieces, (x_ref, *refs) = refs[: cfg.NC], refs[cfg.NC :]
    place_blocks(cfg, idx_ref, x_pieces, x_ref)
    q_ref, k_ref, v_ref, hid_ref, att_ref, lse_ref, bias_ref, w_ref, gain_ref, ah_ref = refs
    assemble(idx_ref, cfg.pair(pieces), w_ref, cfg.rows)
    D, S, hl, CQ = cfg.D, cfg.S, cfg.hl, cfg.CQ
    extra = w_ref[:, 3 * CQ :]
    ew = extra.shape[1]
    pick = b16((iota((16, ew), 0) == iota((16, ew), 1)).astype(jnp.float32))
    gain_rows = dot(pick, extra, NT)
    gain_ref[...] = gain_rows[0:8]
    unit, _ = rms(f32(x_ref[...]))
    hidden = b16(unit * gain_rows[0:1])
    hid_ref[...] = hidden
    qkv = dot(hidden, w_ref[:, : 3 * CQ])
    for h in range(hl):
        q_ref[h] = b16(qkv[:, h * HD : (h + 1) * HD] * SCALE)
        k_ref[h] = b16(qkv[:, CQ + h * HD : CQ + (h + 1) * HD])
        v_ref[h] = b16(qkv[:, 2 * CQ + h * HD : 2 * CQ + (h + 1) * HD])
    table = dot(b16(table_select(cfg.NB, D, cfg.rows, cfg.NE).astype(jnp.float32)), extra)
    lane, col = iota((ew, 16), 0), iota((ew, 16), 1)
    head = idx_ref[0] * hl + col
    mine = (lane == 2 + head) & (col < hl) & (head < cfg.H)
    table = dot(b16(table), b16(mine.astype(jnp.float32)))
    hot = b16((iota((cfg.NB, S), 0) == bucket_ref[...]).astype(jnp.float32))
    offset_bias = dot(b16(table), hot, TN)
    nb = S // TILE
    keep = iota((TILE, TILE), 0) >= iota((TILE, TILE), 1)
    for h in range(hl):
        for k in range(nb):
            now = offset_bias[h : h + 1, k * TILE : (k + 1) * TILE]
            before = offset_bias[h : h + 1, (k - 1) * TILE : k * TILE] if k else now
            row = jnp.concatenate([now, before], axis=1)
            turned = pltpu.roll(
                jnp.broadcast_to(row, (TILE, 2 * TILE)), 0, 1, stride=1, stride_axis=0
            )
            tile = jnp.transpose(turned[:, :TILE])
            bias_ref[h, k] = jnp.where(keep, tile, NEG) if k == 0 else tile

    def one_head(h, carry):
        for ib in range(nb):
            n = (ib + 1) * TILE
            s = dot(q_ref[h, ib * TILE : n], k_ref[h, 0:n], NT)
            s = s + jnp.concatenate([bias_ref[h, ib - jb] for jb in range(ib + 1)], axis=1)
            peak = jnp.max(s, axis=1, keepdims=True)
            lse = peak + jnp.log(jnp.sum(jnp.exp(s - peak), axis=1, keepdims=True))
            lse_ref[h, ib * TILE : n] = lse
            ah_ref[h, ib * TILE : n] = dot(b16(jnp.exp(s - lse)), v_ref[h, 0:n])
        return carry

    lax.fori_loop(0, hl, one_head, 0)
    for h in range(hl):
        att_ref[:, h * HD : (h + 1) * HD] = b16(ah_ref[h])


def slots_of(ids, experts):
    n = ids.shape[0]
    first, second = ids[:, 0:1], ids[:, 1:2]
    e = iota((n, experts), 1)
    hot_a, hot_b = (e == first).astype(jnp.float32), (e == second).astype(jnp.float32)
    earlier = (iota((n, n), 0) > iota((n, n), 1)).astype(jnp.float32)
    count = dot(b16(earlier), b16(hot_a + hot_b))
    slot_a = first * CAP + jnp.sum(count * hot_a, axis=1, keepdims=True).astype(jnp.int32)
    slot_b = second * CAP + jnp.sum(count * hot_b, axis=1, keepdims=True).astype(jnp.int32)
    return slot_a, slot_b


def hot_slots(slot, start, width):
    return (slot == start + iota((slot.shape[0], width), 1)).astype(jnp.float32)


def send_upstream(cfg, idx_ref, ids_ref, up_ref, *outs):
    ids = ids_ref[...]
    slot_a, slot_b = slots_of(ids, cfg.E)
    n = cfg.XC
    other_a = b16(jnp.broadcast_to(f32(ids[:, 1:2]), (cfg.B, EXTRA)))
    other_b = b16(jnp.broadcast_to(f32(ids[:, 0:1]), (cfg.B, EXTRA)))
    for k in range(cfg.NE):
        start = (idx_ref[1] ^ k) * n
        hot_a, hot_b = hot_slots(slot_a, start, n), hot_slots(slot_b, start, n)
        outs[k][:, : cfg.D] = b16(dot(b16(hot_a + hot_b), up_ref[...], TN))
        outs[k][:, cfg.D :] = b16(dot(b16(hot_a), other_a, TN) + dot(b16(hot_b), other_b, TN))


def middle(cfg, idx_ref, x_ref, ids_ref, gain_ref, *refs):
    n_in = len(cfg.orders)
    atts, refs = refs[: cfg.NC], refs[cfg.NC :]
    pieces = refs[:n_in]
    mixed_ref, wo_ref, router_ref = refs[n_in : n_in + 3]
    outs = refs[n_in + 3 : n_in + 3 + cfg.NE]
    w_ref = refs[-1]
    assemble(idx_ref, cfg.pair(pieces), w_ref, cfg.rows)
    D, CQ = cfg.D, cfg.CQ
    wo_ref[0:D, :] = w_ref[:, :D]
    if cfg.NC * CQ > D:
        wo_ref[D:, :] = jnp.zeros((cfg.NC * CQ - D, D), jnp.bfloat16)
    router_ref[...] = w_ref[:, D : D + cfg.E]
    mixed = f32(x_ref[...])
    start = pl.multiple_of(idx_ref[0] * cfg.B, cfg.B)
    for k in range(cfg.NC):
        heads = pl.multiple_of((idx_ref[0] ^ k) * CQ, CQ)
        mixed = mixed + dot(atts[k][pl.ds(start, cfg.B), :], wo_ref[pl.ds(heads, CQ), :])
    mixed_ref[...] = mixed
    unit, _ = rms(mixed)
    hidden = b16(unit * gain_ref[1:2, :])
    slot_a, slot_b = slots_of(ids_ref[...], cfg.E)
    n = cfg.XC
    for k in range(cfg.NE):
        start = (idx_ref[1] ^ k) * n
        hot = hot_slots(slot_a, start, n) + hot_slots(slot_b, start, n)
        outs[k][...] = b16(dot(b16(hot), hidden, TN))


def arrange(cfg, order_ref, *refs):
    pieces, outs = refs[: cfg.NE], refs[cfg.NE :]
    rows = jnp.concatenate([p[...] for p in pieces], axis=0)
    total = rows.shape[0]
    part = total // HALVES
    for n, out in enumerate(outs):
        hot = (iota((part, total), 0) + n * part == order_ref[...]).astype(jnp.float32)
        out[...] = b16(dot(b16(hot), rows))


def gather_sum(cfg, order_ref, *refs):
    ins, outs = refs[: HALVES * cfg.NC], refs[HALVES * cfg.NC :]
    halves = []
    for n in range(HALVES):
        group = ins[n * cfg.NC : (n + 1) * cfg.NC]
        total = f32(group[0][...])
        for piece in group[1:]:
            total = total + f32(piece[...])
        halves.append(b16(total))
    rows = jnp.concatenate(halves, axis=0)
    count = rows.shape[0]
    hot = (iota((count, count), 0) == order_ref[...]).astype(jnp.float32)
    back = b16(dot(b16(hot), rows, TN))
    for k, out in enumerate(outs):
        out[...] = back[k * cfg.XC : (k + 1) * cfg.XC]


def collect(cfg, idx_ref, ids, pieces):
    slot_a, slot_b = slots_of(ids, cfg.E)
    total = None
    for k, piece in enumerate(pieces):
        start = (idx_ref[1] ^ k) * cfg.XC
        hot = hot_slots(slot_a, start, cfg.XC) + hot_slots(slot_b, start, cfg.XC)
        term = dot(b16(hot), piece[...])
        total = term if total is None else total + term
    return total


def finish_forward(cfg, idx_ref, ids_ref, mixed_ref, *refs):
    refs[-1][...] = mixed_ref[...] + collect(cfg, idx_ref, ids_ref[...], refs[:-1])


def moe_back(cfg, idx_ref, ids_ref, mixed_ref, gain_ref, up_ref, *refs):
    pieces = refs[: cfg.NE]
    mix_ref, half_ref, gg_ref = refs[cfg.NE :]
    grad = collect(cfg, idx_ref, ids_ref[...], pieces)
    unit, inverse = rms(mixed_ref[...])
    gg_ref[...] = jnp.broadcast_to(jnp.sum(grad * unit, axis=0, keepdims=True), (8, cfg.D))
    scaled = grad * gain_ref[1:2, :]
    moved = inverse * (scaled - unit * jnp.mean(scaled * unit, axis=-1, keepdims=True))
    grad_mixed = f32(up_ref[...]) + moved
    mix_ref[...] = grad_mixed
    half_ref[...] = b16(grad_mixed)


def expert_kernel(cfg, first, idx_ref, *refs):
    NC, D, E = cfg.NC, cfg.D, cfg.E
    rows_in, ups_in = refs[:NC], refs[NC : 2 * NC]
    win_ref, wout_ref, router_ref = refs[2 * NC : 2 * NC + 3]
    outs = refs[2 * NC + 3 :]
    back, fwd = outs[:NC], outs[NC : 2 * NC]
    rows_out, up_out, act_out, pre_out, route_out = outs[2 * NC :]
    step = pl.program_id(0)
    own = idx_ref[1] * cfg.X + first + step
    rows = jnp.concatenate([r[...] for r in rows_in], axis=0)
    ups = jnp.concatenate([u[...] for u in ups_in], axis=0)
    count = rows.shape[0]
    win, wout = win_ref[0], wout_ref[0]
    other = ups[:, D : D + 1].astype(jnp.float32).astype(jnp.int32)
    up = f32(ups[:, :D])
    lane = iota((count, E), 1)
    is_own = (lane == own).astype(jnp.float32)
    is_other = (lane == other).astype(jnp.float32)
    sign = is_own - is_other
    gap = jnp.sum(dot(rows, router_ref[...]) * sign, axis=1, keepdims=True)
    gate = jax.nn.sigmoid(gap)
    against = jax.nn.sigmoid(-gap)
    up_rows = b16(gate * up)
    preact = dot(rows, win)
    cdf = 0.5 * (1.0 + lax.erf(preact * INV_ROOT_TWO))
    slope = cdf + preact * jnp.exp(-0.5 * preact * preact) * INV_ROOT_TAU
    active = b16(preact * cdf)
    part = dot(active, wout)
    grad_pre = b16(dot(up_rows, wout, NT) * slope)
    weight = gate * against * jnp.sum(up * part, axis=1, keepdims=True)
    coef = weight * sign
    high = b16(coef)
    low = b16(coef - f32(high))
    route_ref = router_ref[...]
    both = jnp.concatenate([f32(high), f32(low)], axis=1).astype(jnp.bfloat16)
    wide = jnp.concatenate([f32(route_ref), f32(route_ref)], axis=1).astype(jnp.bfloat16)
    back_rows = dot(grad_pre, win, NT) + dot(both, wide, NT)
    route = dot(rows, both, TN)

    @pl.when(step == 0)
    def _():
        route_out[...] = route

    @pl.when(step > 0)
    def _():
        route_out[...] += route

    fwd_rows = b16(gate * part)
    back_rows = b16(back_rows)
    each = count // NC
    for c in range(NC):
        back[c][...] = back_rows[c * each : (c + 1) * each]
        fwd[c][...] = fwd_rows[c * each : (c + 1) * each]
    rows_out[0] = rows
    up_out[0] = up_rows
    act_out[0] = active
    pre_out[0] = grad_pre


def experts(cfg, half, idx, rows, ups, w_in, w_out, router):
    NC, D, FL = cfg.NC, cfg.D, w_in.shape[2]
    steps = cfg.X // HALVES
    first = half * steps
    each = cfg.NE * CAP
    count = NC * each
    fixed = lambda shape: pl.BlockSpec(shape, lambda s: (0,) * len(shape))
    row = lambda w: pl.BlockSpec((each, w), lambda s: (s, 0))
    per = lambda a, b: pl.BlockSpec((1, a, b), lambda s: (first + s, 0, 0))
    here = lambda a, b: pl.BlockSpec((1, a, b), lambda s: (s, 0, 0))
    saved = [((steps, count, w), jnp.bfloat16) for w in (D, D, FL, FL)]
    outs = [((steps * each, D), jnp.bfloat16)] * (2 * NC) + saved + [((D, 2 * cfg.E), jnp.float32)]
    in_specs = [SMEM] + [row(D)] * NC + [row(D + EXTRA)] * NC
    in_specs += [per(D, FL), per(FL, D), fixed((D, cfg.E))]
    out_specs = [row(D)] * (2 * NC) + [here(count, w) for w in (D, D, FL, FL)]
    out_specs += [fixed((D, 2 * cfg.E))]
    return pl.pallas_call(
        functools.partial(expert_kernel, cfg, first),
        grid=(steps,),
        out_shape=[jax.ShapeDtypeStruct(s, d) for s, d in outs],
        in_specs=in_specs,
        out_specs=out_specs,
        cost_estimate=pl.CostEstimate(
            flops=steps * 4 * 2 * count * D * FL, bytes_accessed=steps * 4 * D * FL, transcendentals=0
        ),
    )(idx, *rows, *ups, w_in, w_out, router)


def expert_weights_kernel(rows_ref, up_ref, act_ref, pre_ref, *refs):
    gin_ref, gout_ref = refs[-2:]
    gin_ref[0] = dot(rows_ref[0], pre_ref[0], TN)
    gout_ref[0] = dot(act_ref[0], up_ref[0], TN)


def expert_weights(cfg, half, rows, up, act, pre, earlier):
    steps, count, D = rows.shape
    FL = act.shape[2]
    here = lambda a, b: pl.BlockSpec((1, a, b), lambda s: (s, 0, 0))
    per = lambda a, b: pl.BlockSpec((1, a, b), lambda s: (half * steps + s, 0, 0))
    return pl.pallas_call(
        expert_weights_kernel,
        grid=(steps,),
        out_shape=[
            jax.ShapeDtypeStruct((cfg.X, D, FL), jnp.float32),
            jax.ShapeDtypeStruct((cfg.X, FL, D), jnp.float32),
        ],
        in_specs=[here(count, D), here(count, D), here(count, FL), here(count, FL)]
        + [pl.BlockSpec(memory_space=pl.ANY)] * len(earlier),
        out_specs=[per(D, FL), per(FL, D)],
        input_output_aliases={4 + n: n for n in range(len(earlier))},
        cost_estimate=pl.CostEstimate(
            flops=steps * 4 * count * D * FL, bytes_accessed=steps * 8 * D * FL, transcendentals=0
        ),
    )(rows, up, act, pre, *earlier)


def attn_backward(
    cfg, idx_ref, x_ref, bucket_ref, wo_ref, q_ref, k_ref, v_ref, hid_ref, lse_ref,
    bias_ref, w_ref, gain_ref, gg_ref, *refs,
):
    NC = cfg.NC
    routes, refs = refs[:HALVES], refs[HALVES:]
    gm_in, atts, refs = refs[:NC], refs[NC : 2 * NC], refs[2 * NC :]
    mine_ref, part_ref, *gh_out = refs[: 2 + NC]
    da_ref, dq_ref, dk_ref, dv_ref, p_ref, ds_ref, acc_ref, dw_ref, gm_ref, gh_ref = refs[2 + NC :]
    D, S, hl, CQ, CO, B = cfg.D, cfg.S, cfg.hl, cfg.CQ, cfg.CO, cfg.B
    nb = S // TILE
    c = idx_ref[0]
    place_blocks(cfg, idx_ref, gm_in, gm_ref)
    gm = gm_ref[...]
    own = pl.multiple_of(c * CQ, CQ)
    grad_att = b16(dot(gm, wo_ref[pl.ds(own, CQ), :], NT))
    for h in range(hl):
        da_ref[h] = grad_att[:, h * HD : (h + 1) * HD]
    prod = f32(grad_att) * f32(atts[0][...])
    deltas = [jnp.sum(prod[:, h * HD : (h + 1) * HD], axis=1, keepdims=True) for h in range(hl)]
    acc_ref[...] = jnp.zeros_like(acc_ref)
    for ib in range(nb):
        if ib + 1 < nb:
            zero = jnp.zeros((TILE, S - (ib + 1) * TILE), jnp.bfloat16)
            p_ref[ib * TILE : (ib + 1) * TILE, (ib + 1) * TILE :] = zero
            ds_ref[ib * TILE : (ib + 1) * TILE, (ib + 1) * TILE :] = zero
    for h in range(hl):
        for ib in range(nb):
            lo, n = ib * TILE, (ib + 1) * TILE
            s = dot(q_ref[h, lo:n], k_ref[h, 0:n], NT)
            s = s + jnp.concatenate([bias_ref[h, ib - jb] for jb in range(ib + 1)], axis=1)
            prob = jnp.exp(s - lse_ref[h, lo:n])
            grad_p = dot(da_ref[h, lo:n], v_ref[h, 0:n], NT)
            grad_s = prob * (grad_p - deltas[h][lo:n])
            p_ref[lo:n, 0:n] = b16(prob)
            half = b16(grad_s)
            ds_ref[lo:n, 0:n] = half
            dq_ref[h, lo:n] = dot(half, k_ref[h, 0:n]) * SCALE
            for jb in range(ib + 1):
                acc_ref[h, ib - jb] += grad_s[:, jb * TILE : (jb + 1) * TILE]
        dk_ref[h] = dot(ds_ref[...], q_ref[h], TN)
        dv_ref[h] = dot(p_ref[...], da_ref[h], TN)
    per_offset = []
    zero_tile = jnp.zeros((TILE, TILE), jnp.float32)
    sub = iota((8, 2 * TILE), 0)
    for h in range(hl):
        rows = []
        for k in range(nb):
            wide = jnp.concatenate([jnp.transpose(acc_ref[h, k]), zero_tile], axis=1)
            total = wide[0:8]
            for g in range(1, TILE // 8):
                total = total + pltpu.roll(wide[g * 8 : (g + 1) * 8], 2 * TILE - 8 * g, 1)
            for bit in (1, 2, 4):
                total = jnp.where((sub & bit) != 0, pltpu.roll(total, 2 * TILE - bit, 1), total)
            rows.append(jnp.sum(total, axis=0, keepdims=True))
        spans = []
        for k in range(nb):
            span = rows[k][:, :TILE]
            if k + 1 < nb:
                span = span + rows[k + 1][:, TILE:]
            spans.append(span)
        per_offset.append(jnp.concatenate(spans, axis=1))
    per_offset.append(jnp.zeros((8 - hl, S), jnp.float32))
    per_offset = jnp.concatenate(per_offset, axis=0)
    hot = (iota((cfg.NB, S), 0) == bucket_ref[...]).astype(jnp.float32)
    table = dot(per_offset, hot, NT, lax.Precision.HIGHEST)
    place = table_select(cfg.NB, D, cfg.rows, cfg.NE).astype(jnp.float32)
    table_rows = dot(table, place, NN, lax.Precision.HIGHEST)
    grads = jnp.concatenate(
        [dq_ref[h] for h in range(hl)] + [dk_ref[h] for h in range(hl)] + [dv_ref[h] for h in range(hl)],
        axis=1,
    )
    grads = b16(grads)
    dw_ref[0:D, : 3 * CQ] = dot(hid_ref[...], grads, TN)
    sel = b16((iota((D, CO), 0) == c * CO + iota((D, CO), 1)).astype(jnp.float32))
    gm_cols = b16(dot(gm, sel))
    for k in range(NC):
        heads = pl.multiple_of((c ^ k) * CQ, CQ)
        dw_ref[pl.ds(heads, CQ), 3 * CQ : 3 * CQ + CO] = dot(atts[k][...], gm_cols, TN)
    gh = dot(grads, w_ref[:, : 3 * CQ], NT)
    gh_ref[...] = b16(gh)
    for k, out in enumerate(gh_out):
        out[...] = gh_ref[pl.ds(pl.multiple_of((c ^ k) * B, B), B), :]
    unit, _ = rms(f32(x_ref[...]))
    gain_one = jnp.sum(gh * unit, axis=0, keepdims=True)
    E = cfg.E
    stack = jnp.concatenate(
        [
            jnp.zeros((E, D), jnp.float32),
            gain_one,
            gg_ref[0:1, :],
            table_rows[0:hl],
            jnp.zeros((EXTRA - E - 2 - hl, D), jnp.float32),
        ],
        axis=0,
    )
    extra = jnp.transpose(stack)
    route = routes[0][...]
    for r in routes[1:]:
        route = route + r[...]
    route = route[:, :E] + route[:, E:]
    extra = extra + jnp.concatenate([route, jnp.zeros((D, EXTRA - E), jnp.float32)], axis=1)
    dw_ref[0:D, 3 * CQ + CO :] = extra
    me = idx_ref[1]
    R = cfg.rows
    for j in range(cfg.NE // 2):
        a = pl.multiple_of((me ^ (2 * j)) * R, R)
        b = pl.multiple_of((me ^ (2 * j + 1)) * R, R)
        mine_ref[j * R : (j + 1) * R, :] = b16(dw_ref[pl.ds(a, R), :])
        part_ref[j * R : (j + 1) * R, :] = b16(dw_ref[pl.ds(b, R), :])


def add_pairs(cfg, a_ref, b_ref, *outs):
    R = cfg.rows
    for j, out in enumerate(outs):
        out[...] = b16(f32(a_ref[j * R : (j + 1) * R]) + f32(b_ref[j * R : (j + 1) * R]))


def add_all(*refs):
    total = f32(refs[0][...])
    for r in refs[1:-1]:
        total = total + f32(r[...])
    refs[-1][...] = b16(total)


def last_input(x_ref, gain_ref, mix_ref, *refs):
    out_ref = refs[-1]
    total = f32(refs[0][...])
    for ref in refs[1:-1]:
        total = total + f32(ref[...])
    unit, inverse = rms(f32(x_ref[...]))
    scaled = total * gain_ref[0:1, :]
    moved = inverse * (scaled - unit * jnp.mean(scaled * unit, axis=-1, keepdims=True))
    out_ref[...] = mix_ref[...] + moved


def last_weights(cfg, all_ref, q_ref, k_ref, v_ref, o_ref, router_ref, one_ref, two_ref, table_ref):
    R, CQ, CO, D, hl, E = cfg.rows, cfg.CQ, cfg.CO, cfg.D, cfg.hl, cfg.E
    pieces = [f32(all_ref[n * R : (n + 1) * R, :]) for n in range(cfg.NC)]
    for t, ref in enumerate((q_ref, k_ref, v_ref)):
        full = jnp.concatenate([p[:, t * CQ : (t + 1) * CQ] for p in pieces], axis=1)
        ref[...] = full[:, :D]
    o_ref[...] = jnp.concatenate([p[:, 3 * CQ : 3 * CQ + CO] for p in pieces], axis=1)
    base = 3 * CQ + CO
    extra = pieces[0][:, base:]
    for p in pieces[1:]:
        extra = extra + p[:, base:]
    router_ref[...] = jnp.transpose(extra)[:E]
    eye = (iota((R, R), 0) == iota((R, R), 1)).astype(jnp.float32)
    one_ref[...] = jnp.sum(eye * extra[:, E : E + 1], axis=0, keepdims=True)
    two_ref[...] = jnp.sum(eye * extra[:, E + 1 : E + 2], axis=0, keepdims=True)
    table = jnp.concatenate([p[:, base + E + 2 : base + E + 2 + hl] for p in pieces], axis=1)
    table_ref[...] = table[: cfg.NB // cfg.NE, : cfg.H]


class Config:
    def pair(self, pieces):
        if len(pieces) == 1:
            return list(pieces)
        return list(zip(self.orders, pieces, strict=True))


def permute(x, axis, k, n):
    return lax.ppermute(x, axis, [(i, i ^ k) for i in range(n)])


def spread(first, rest, axis, n):
    return [first] + [permute(x, axis, k, n) for k, x in zip(range(1, n), rest, strict=True)]


def gather_rows(cfg, x):
    if len(cfg.orders) == 1:
        return [lax.all_gather(x, "ep", axis=0, tiled=True)]
    got = [x] + [permute(x, "ep", 2 * j, cfg.NE) for j in range(1, cfg.NE // 2)]
    return got + [permute(g, "ep", 1, cfg.NE) for g in got]


def body(
    block_input, out_grad, w_query, w_key, w_value, w_output, w_router, attn_gain, moe_gain,
    bias_table, rel_bucket, expert_ids, expert_in, expert_out,
):
    cfg = Config()
    NC, NE = lax.axis_size("ctx"), lax.axis_size("ep")
    B, D = block_input.shape[1:]
    S = rel_bucket.shape[0]
    cfg.NC, cfg.NE, cfg.B, cfg.D, cfg.S = NC, NE, B, D, S
    cfg.H = D // HD
    cfg.hl = -(-cfg.H // NC)
    cfg.CQ = CQ = cfg.hl * HD
    cfg.CO = CO = D // NC
    cfg.rows = R = D // NE
    cfg.X = X = expert_in.shape[0]
    cfg.E = E = X * NE
    cfg.XC = X * CAP
    cfg.NB = bias_table.shape[0] * NE
    hl = cfg.hl
    if R % 16 == 0:
        cfg.orders = [(2 * j,) for j in range(NE // 2)] + [(2 * j + 1,) for j in range(NE // 2)]
    else:
        cfg.orders = [None]
    bf, fl = jnp.bfloat16, jnp.float32
    c, e = lax.axis_index("ctx"), lax.axis_index("ep")
    idx = jnp.stack([c, e]).astype(jnp.int32)
    x_own, up_own, ids = block_input[0], out_grad[0], expert_ids[0]
    bucket = rel_bucket.reshape(1, S)

    W1 = 3 * CQ + HD
    pack_a, pack_b = call(
        functools.partial(pack_weights, cfg),
        [idx, w_query, w_key, w_value, w_output, w_router.T, attn_gain[None], moe_gain[None], bias_table],
        [((R, W1), bf), ((R, D + E), bf)], scratch=[pltpu.VMEM((R, TILE), fl)],
    )
    first = gather_rows(cfg, pack_a)
    x_pieces = spread(x_own, [x_own] * (NC - 1), "ctx", NC)
    second = gather_rows(cfg, pack_b)
    up_send = call(functools.partial(send_upstream, cfg), [idx, ids, up_own], [((cfg.XC, D + EXTRA), bf)] * NE)
    ks = np.arange(E * CAP)
    to = (ks % cfg.XC) // CAP * (NE * CAP) + ks // cfg.XC * CAP + ks % CAP
    order = jnp.asarray(to.reshape(1, -1), jnp.int32)

    def to_experts(sent):
        got = spread(sent[0], sent[1:], "ep", NE)
        w = sent[0].shape[1]
        halves = call(
            functools.partial(arrange, cfg), [order, *got], [((E * CAP // HALVES, w), bf)] * HALVES,
            n_smem=0,
        )
        return [spread(h, [h] * (NC - 1), "ctx", NC) for h in halves]

    def from_experts(parts):
        got = []
        for half in parts:
            got += spread(half[0], half[1:], "ctx", NC)
        sent = call(functools.partial(gather_sum, cfg), [order, *got], [((cfg.XC, D), bf)] * NE, n_smem=0)
        return spread(sent[0], sent[1:], "ep", NE)

    ups = to_experts(up_send)
    nb = S // TILE
    x_all, q, k, v, hidden, att, lse, bias, w_all, gains = call(
        functools.partial(attn_forward, cfg), [idx, bucket, *first, *x_pieces],
        [((S, D), bf)] + [((hl, S, HD), bf)] * 3 + [((S, D), bf), ((S, CQ), bf), ((hl, S, 1), fl), ((hl, nb, TILE, TILE), fl),
         ((D, W1), bf), ((8, D), fl)],
        scratch=[pltpu.VMEM((hl, S, HD), fl)], flops=2e9,
    )
    atts = spread(att, [att] * (NC - 1), "ctx", NC)
    mixed, wo, router, *sent = call(
        functools.partial(middle, cfg), [idx, x_own, ids, gains, *atts, *second],
        [((B, D), fl), ((NC * CQ, D), bf), ((D, E), bf)] + [((cfg.XC, D), bf)] * NE,
        scratch=[pltpu.VMEM((D, D + E), bf)],
    )
    rows = to_experts(sent)
    backs, fwds, routes, grads = [], [], [], []
    for half in range(HALVES):
        got = experts(cfg, half, idx, rows[half], ups[half], expert_in, expert_out, router)
        backs.append(got[:NC])
        fwds.append(got[NC : 2 * NC])
        grads = expert_weights(cfg, half, *got[2 * NC : 2 * NC + 4], grads)
        routes.append(got[-1])
    grad_expert_in, grad_expert_out = grads
    back = from_experts(backs)
    mix, mix_half, gg = call(
        functools.partial(moe_back, cfg), [idx, ids, mixed, gains, up_own, *back],
        [((B, D), fl), ((B, D), bf), ((8, D), fl)],
    )
    fwd = from_experts(fwds)
    (block_output,) = call(functools.partial(finish_forward, cfg), [idx, ids, mixed, *fwd], [((B, D), fl)])
    gm = spread(mix_half, [mix_half] * (NC - 1), "ctx", NC)
    WC = 3 * CQ + CO + EXTRA
    mine, part, *gh = call(
        functools.partial(attn_backward, cfg),
        [idx, x_all, bucket, wo, q, k, v, hidden, lse, bias, w_all, gains, gg, *routes, *gm, *atts],
        [((D // 2, WC), bf)] * 2 + [((B, D), bf)] * NC,
        scratch=[
            pltpu.VMEM((hl, S, HD), bf),
            pltpu.VMEM((hl, S, HD), fl),
            pltpu.VMEM((hl, S, HD), fl),
            pltpu.VMEM((hl, S, HD), fl),
            pltpu.VMEM((S, S), bf),
            pltpu.VMEM((S, S), bf),
            pltpu.VMEM((hl, nb, TILE, TILE), fl),
            pltpu.VMEM((NC * CQ, WC), fl),
            pltpu.VMEM((S, D), bf),
            pltpu.VMEM((S, D), bf),
        ],
        flops=4e9,
    )
    theirs = permute(part, "ep", 1, NE)
    gh = spread(gh[0], gh[1:], "ctx", NC)
    pairs = call(functools.partial(add_pairs, cfg), [mine, theirs], [((R, WC), bf)] * (NE // 2), n_smem=0)
    pairs = [pairs[0]] + [permute(pairs[j], "ep", 2 * j, NE) for j in range(1, NE // 2)]
    (total,) = call(add_all, pairs, [((R, WC), bf)], n_smem=0)
    everyone = lax.all_gather(total, "ctx", axis=0, tiled=True)
    (input_grad,) = call(last_input, [x_own, gains, mix, *gh], [((B, D), fl)], n_smem=0)
    nbl = bias_table.shape[0]
    gq, gk, gv, go, grouter, gone, gtwo, gtable = call(
        functools.partial(last_weights, cfg), [everyone],
        [((R, D), fl)] * 4 + [((E, R), fl), ((1, R), fl), ((1, R), fl), ((nbl, cfg.H), fl)], n_smem=0,
    )
    return (
        block_output[None], input_grad[None], gq, gk, gv, go, grouter.T, gone[0], gtwo[0], gtable,
        grad_expert_in, grad_expert_out,
    )


def solution(mesh):
    two, three = P("ep", None), P("ep", "ctx", None)
    in_specs = (three, three, two, two, two, two, two, P("ep"), P("ep"), two, P(), three, P("ep", None, "ctx"), three)
    out_specs = (three, three, two, two, two, two, two, P("ep"), P("ep"), two, P("ep", None, "ctx"), three)
    return jax.shard_map(body, mesh=mesh, in_specs=in_specs, out_specs=out_specs, check_vma=False)
```

profile of v0, /device:TPU:0, one launch (start us, length us, event | category | flops | bytes accessed | tf_op | source)
XLA Modules:
  0.0 313.4 jit_solution(1171657845601999126)
XLA Ops:
  2.6 2.6 shard_map.242
  5.7 2.6 collective-permute-start.31
  8.4 2.8 collective-permute-start.33
  11.1 2.2 shard_map.238
  13.7 3.8 %collective-permute-start.35 = (bf16[48,896]{1,0:T(8,128)(2,1)}, bf16[48,896]{1,0:T(8,128)(2,1)S(1)}, u32[]{:S(2)}, u32[]{:S(2)}) collective-permute-start(bf16[48,896]{1,0:T(8,128)(2,1)} %get-tuple-element.134), channel_id=1, source_target_pairs={{0,6},{1,7},{2,4},{3,5},{4,2},{5,3},{6,0},{7,1},{8,14},{9,15},{10,... | collective-permute-start | bytes 258056 | tf_op jit(solution)/shard_map/ppermute | solution.py:564
  18.6 9.1 %collective-permute-done.34.refs_5_ = bf16[48,896]{1,0:T(8,128)(2,1)S(1)} collective-permute-done((bf16[48,896]{1,0:T(8,128)(2,1)}, bf16[48,896]{1,0:T(8,128)(2,1)S(1)}, u32[]{:S(2)}, u32[]{:S(2)}) %collective-permute-start.34) | collective-permute-done | bytes 86048 | tf_op jit(solution)/shard_map/ppermute | solution.py:564
  27.7 2.5 collective-permute-start.15
  30.5 2.4 collective-permute-start.9
  34.8 4.9 %collective-permute-done.1.refs_2_ = bf16[96,640]{1,0:T(8,128)(2,1)S(1)} collective-permute-done((bf16[96,640]{1,0:T(8,128)(2,1)}, bf16[96,640]{1,0:T(8,128)(2,1)S(1)}, u32[]{:S(2)}, u32[]{:S(2)}) %collective-permute-start.1) | collective-permute-done | bytes 122912 | tf_op jit(solution)/shard_map/ppermute | solution.py:564
  44.3 5.5 %collective-permute-done.14.refs_6_ = bf16[96,832]{1,0:T(8,128)(2,1)S(1)} collective-permute-done((bf16[96,832]{1,0:T(8,128)(2,1)}, bf16[96,832]{1,0:T(8,128)(2,1)S(1)}, u32[]{:S(2)}, u32[]{:S(2)}) %collective-permute-start.14) | collective-permute-done | bytes 159776 | tf_op jit(solution)/shard_map/ppermute | solution.py:564
  50.8 2.5 collective-permute-start.36
  54.5 9.7 %shard_map.239 = (bf16[512,768]{1,0:T(8,128)(2,1)}, bf16[3,512,64]{2,1,0:T(8,128)(2,1)}, bf16[3,512,64]{2,1,0:T(8,128)(2,1)}, bf16[3,512,64]{2,1,0:T(8,128)(2,1)...) custom-call(s32[2]{0:T(128)} %pad_add_fusion.idx_ref, ...), custom_call_target="tpu_custom_call" | custom-call | flops 2000000000 | bytes 5931016 | tf_op jit(solution)/shard_map/pallas_call | solution.py:53
  64.2 2.5 collective-permute-start.12
  67.8 2.5 shard_map.243
  70.3 2.5 collective-permute-start.39
  74.6 5.5 %collective-permute-done.11.refs_2_.refs_8_ = bf16[512,192]{1,0:T(8,128)(2,1)S(1)} collective-permute-done((bf16[512,192]{1,0:T(8,128)(2,1)}, bf16[512,192]{1,0:T(8,128)(2,1)S(1)}, u32[]{:S(2)}, u32[]{:S(2)}) %collective-permute-start.11) | collective-permute-done | bytes 196640 | tf_op jit(solution)/shard_map/ppermute | solution.py:564
  81.0 3.7 %shard_map.240 = (f32[128,768]{1,0:T(8,128)}, bf16[768,768]{1,0:T(8,128)(2,1)}, bf16[768,64]{1,0:T(8,128)(2,1)}, bf16[48,768]{1,0:T(8,128)(2,1)}, bf16[48,768]{1...) custom-call(s32[2]{0:T(128)} %pad_add_fusion.idx_ref, ...), custom_call_target="tpu_custom_call" | custom-call | flops 100000000 | bytes 4547592 | tf_op jit(solution)/shard_map/pallas_call | solution.py:53
  101.3 2.3 shard_map.241
  111.6 5.7 %collective-permute-done.45.refs_3_ = bf16[192,768]{1,0:T(8,128)(2,1)S(1)} collective-permute-done((bf16[192,768]{1,0:T(8,128)(2,1)}, bf16[192,768]{1,0:T(8,128)(2,1)S(1)}, u32[]{:S(2)}, u32[]{:S(2)}) %collective-permute-start.45) | collective-permute-done | bytes 294944 | tf_op jit(solution)/shard_map/ppermute | solution.py:564
  118.9 2.4 collective-permute-done.44.refs_2_
  124.3 12.1 %shard_map.245 = (bf16[192,768]{1,0:T(8,128)(2,1)}, bf16[192,768]{1,0:T(8,128)(2,1)}, bf16[192,768]{1,0:T(8,128)(2,1)}, bf16[192,768]{1,0:T(8,128)(2,1)}, bf16[1...) custom-call(s32[2]{0:T(128)} %pad_add_fusion.idx_ref, ...), custom_call_target="tpu_custom_call" | custom-call | flops 3623878656 | bytes 9437184 | tf_op jit(solution)/shard_map/pallas_call | solution.py:361
  143.6 12.2 %shard_map.244 = (bf16[192,768]{1,0:T(8,128)(2,1)}, bf16[192,768]{1,0:T(8,128)(2,1)}, bf16[192,768]{1,0:T(8,128)(2,1)}, bf16[192,768]{1,0:T(8,128)(2,1)}, bf16[1...) custom-call(s32[2]{0:T(128)} %pad_add_fusion.idx_ref, ...), custom_call_target="tpu_custom_call" | custom-call | flops 3623878656 | bytes 9437184 | tf_op jit(solution)/shard_map/pallas_call | solution.py:361
  159.4 6.2 %collective-permute-done.59.refs_1_ = bf16[192,768]{1,0:T(8,128)(2,1)S(1)} collective-permute-done((bf16[192,768]{1,0:T(8,128)(2,1)}, bf16[192,768]{1,0:T(8,128)(2,1)S(1)}, u32[]{:S(2)}, u32[]{:S(2)}) %collective-permute-start.59) | collective-permute-done | bytes 294944 | tf_op jit(solution)/shard_map/ppermute | solution.py:564
  165.6 4.4 %collective-permute-done.60.refs_2_ = bf16[192,768]{1,0:T(8,128)(2,1)S(1)} collective-permute-done((bf16[192,768]{1,0:T(8,128)(2,1)}, bf16[192,768]{1,0:T(8,128)(2,1)S(1)}, u32[]{:S(2)}, u32[]{:S(2)}) %collective-permute-start.60) | collective-permute-done | bytes 294944 | tf_op jit(solution)/shard_map/ppermute | solution.py:564
  170.9 3.0 shard_map.248
  173.9 4.0 %collective-permute-start.66 = (bf16[48,768]{1,0:T(8,128)(2,1)}, bf16[48,768]{1,0:T(8,128)(2,1)S(1)}, u32[]{:S(2)}, u32[]{:S(2)}) collective-permute-start(bf16[48,768]{1,0:T(8,128)(2,1)} %get-tuple-element.166), channel_id=1, source_target_pairs={{0,2},{1,3},{2,0},{3,1},{4,6},{5,7},{6,4},{7,5},{8,10},{9,11},{10,... | collective-permute-start | bytes 221192 | tf_op jit(solution)/shard_map/ppermute | solution.py:564
  180.4 3.1 %collective-permute-start.70 = (bf16[48,768]{1,0:T(8,128)(2,1)}, bf16[48,768]{1,0:T(8,128)(2,1)S(1)}, u32[]{:S(2)}, u32[]{:S(2)}) collective-permute-start(bf16[48,768]{1,0:T(8,128)(2,1)} %get-tuple-element.170), channel_id=1, source_target_pairs={{0,6},{1,7},{2,4},{3,5},{4,2},{5,3},{6,0},{7,1},{8,14},{9,15},{10,... | collective-permute-start | bytes 221192 | tf_op jit(solution)/shard_map/ppermute | solution.py:564
  184.2 7.7 %collective-permute-done.69.refs_5_ = bf16[48,768]{1,0:T(8,128)(2,1)S(1)} collective-permute-done((bf16[48,768]{1,0:T(8,128)(2,1)}, bf16[48,768]{1,0:T(8,128)(2,1)S(1)}, u32[]{:S(2)}, u32[]{:S(2)}) %collective-permute-start.69) | collective-permute-done | bytes 73760 | tf_op jit(solution)/shard_map/ppermute | solution.py:564
  192.5 3.2 %shard_map.249 = (f32[128,768]{1,0:T(8,128)}, bf16[128,768]{1,0:T(8,128)(2,1)}, f32[8,768]{1,0:T(8,128)}) custom-call(s32[2]{0:T(128)} %pad_add_fusion.idx_ref, s32[128,2]{1,0:T(8,128)} %bitcast.16, f32[128,768]{1,0:T(8,128)} %get-tuple-element.118.mixed_ref, f32[8,768]{1,0:T(8,128)} %get-tuple-element.115.gain_ref, bf16[128,768]{1,0:T(8,128)(2,1)} %bitcast.27, ...), custom_call_target="tpu_custom_call" | custom-call | flops 100000000 | bytes 1819656 | tf_op jit(solution)/shard_map/pallas_call | solution.py:53
  201.3 3.4 %collective-permute-done.74.refs_5_ = bf16[128,768]{1,0:T(8,128)(2,1)S(1)} collective-permute-done((bf16[128,768]{1,0:T(8,128)(2,1)}, bf16[128,768]{1,0:T(8,128)(2,1)S(1)}, u32[]{:S(2)}, u32[]{:S(2)}) %collective-permute-start.74) | collective-permute-done | bytes 196640 | tf_op jit(solution)/shard_map/ppermute | solution.py:564
  204.7 3.4 %collective-permute-done.73.refs_4_ = bf16[128,768]{1,0:T(8,128)(2,1)S(1)} collective-permute-done((bf16[128,768]{1,0:T(8,128)(2,1)}, bf16[128,768]{1,0:T(8,128)(2,1)S(1)}, u32[]{:S(2)}, u32[]{:S(2)}) %collective-permute-start.73) | collective-permute-done | bytes 196640 | tf_op jit(solution)/shard_map/ppermute | solution.py:564
  208.8 11.7 %shard_map.250 = (bf16[384,896]{1,0:T(8,128)(2,1)}, bf16[384,896]{1,0:T(8,128)(2,1)}, bf16[128,768]{1,0:T(8,128)(2,1)}, bf16[128,768]{1,0:T(8,128)(2,1)}, bf16[1...) custom-call(s32[2]{0:T(128)} %pad_add_fusion.idx_ref, bf16[512,768]{1,0:T(8,128)(2,1)} %get-tuple-element.173.x_ref, ...), custom_call_target="tpu_custom_call" | custom-call | flops 4000000000 | bytes 9691144 | tf_op jit(solution)/shard_map/pallas_call | solution.py:53
  226.2 5.3 %collective-permute-done.51.refs_7_ = bf16[192,768]{1,0:T(8,128)(2,1)S(1)} collective-permute-done((bf16[192,768]{1,0:T(8,128)(2,1)S(1)}, bf16[192,768]{1,0:T(8,128)(2,1)S(1)}, u32[]{:S(2)}, u32[]{:S(2)}) %collective-permute-start.51) | collective-permute-done | bytes 294944 | tf_op jit(solution)/shard_map/ppermute | solution.py:564
  231.5 6.2 %collective-permute-done.40.refs_1_ = bf16[192,768]{1,0:T(8,128)(2,1)S(1)} collective-permute-done((bf16[192,768]{1,0:T(8,128)(2,1)}, bf16[192,768]{1,0:T(8,128)(2,1)S(1)}, u32[]{:S(2)}, u32[]{:S(2)}) %collective-permute-start.40) | collective-permute-done | bytes 294944 | tf_op jit(solution)/shard_map/ppermute | solution.py:564
  237.7 5.9 %collective-permute-done.42.refs_3_ = bf16[192,768]{1,0:T(8,128)(2,1)S(1)} collective-permute-done((bf16[192,768]{1,0:T(8,128)(2,1)S(1)}, bf16[192,768]{1,0:T(8,128)(2,1)S(1)}, u32[]{:S(2)}, u32[]{:S(2)}) %collective-permute-start.42) | collective-permute-done | bytes 294944 | tf_op jit(solution)/shard_map/ppermute | solution.py:564
  244.3 3.0 shard_map.246
  247.3 3.7 %collective-permute-start.53 = (bf16[48,768]{1,0:T(8,128)(2,1)}, bf16[48,768]{1,0:T(8,128)(2,1)S(1)}, u32[]{:S(2)}, u32[]{:S(2)}) collective-permute-start(bf16[48,768]{1,0:T(8,128)(2,1)} %get-tuple-element.150), channel_id=1, source_target_pairs={{0,2},{1,3},{2,0},{3,1},{4,6},{5,7},{6,4},{7,5},{8,10},{9,11},{10,... | collective-permute-start | bytes 221192 | tf_op jit(solution)/shard_map/ppermute | solution.py:564
  251.1 2.6 collective-permute-start.55
  257.0 2.4 collective-permute-start.57
  260.4 3.3 %collective-permute-done.56.refs_5_ = bf16[48,768]{1,0:T(8,128)(2,1)S(1)} collective-permute-done((bf16[48,768]{1,0:T(8,128)(2,1)}, bf16[48,768]{1,0:T(8,128)(2,1)S(1)}, u32[]{:S(2)}, u32[]{:S(2)}) %collective-permute-start.56) | collective-permute-done | bytes 73760 | tf_op jit(solution)/shard_map/ppermute | solution.py:564
  263.8 2.8 collective-permute-start.77
  266.6 8.8 %shard_map.255 = (f32[8,768,768]{2,1,0:T(8,128)}, f32[8,768,768]{2,1,0:T(8,128)}) custom-call(bf16[4,192,768]{2,1,0:T(8,128)(2,1)} %get-tuple-element.208.rows_ref, bf16[4,192,768]{2,1,0:T(8,128)(2,1)} %get-tuple-element.209.up_ref, bf16[4,192,768]{2,1,0:T(8,128)(2,1)} %get-tuple-element.210.act_ref, bf16[4,192,768]{2,1,0:T(8,128)(2,1)} %get-tuple-element.211.pre_ref), custom_call_target="tpu_custom_call" | custom-call | flops 1811939328 | bytes 18874368 | tf_op jit(solution)/shard_map/pallas_call | solution.py:384
  278.2 3.9 %collective-permute-start.81 = (bf16[96,896]{1,0:T(8,128)(2,1)}, bf16[96,896]{1,0:T(8,128)(2,1)S(1)}, u32[]{:S(2)}, u32[]{:S(2)}) collective-permute-start(bf16[96,896]{1,0:T(8,128)(2,1)} %get-tuple-element.195), channel_id=1, source_target_pairs={{0,6},{1,7},{2,4},{3,5},{4,2},{5,3},{6,0},{7,1},{8,14},{9,15},{10,... | collective-permute-start | bytes 516104 | tf_op jit(solution)/shard_map/ppermute | solution.py:564
  282.1 8.8 %shard_map.256 = (f32[8,768,768]{2,1,0:T(8,128)}, f32[8,768,768]{2,1,0:T(8,128)}) custom-call(bf16[4,192,768]{2,1,0:T(8,128)(2,1)} %get-tuple-element.204.rows_ref, bf16[4,192,768]{2,1,0:T(8,128)(2,1)} %get-tuple-element.205.up_ref, bf16[4,192,768]{2,1,0:T(8,128)(2,1)} %get-tuple-element.206.act_ref, ...), custom_call_target="tpu_custom_call", output_to_operand_aliasing={{0}: (4, {}), {1}: (5, {})} | custom-call | flops 1811939328 | bytes 18874368 | tf_op jit(solution)/shard_map/pallas_call | solution.py:384
  291.0 2.9 shard_map.247
  294.6 2.4 shard_map.251
  299.8 11.4 %all_gather.3.all_ref = bf16[384,896]{1,0:T(8,128)(2,1)} all-gather(bf16[96,896]{1,0:T(8,128)(2,1)} %shard_map.253), channel_id=1, replica_groups=mesh['ctx'=4,'ep'=8] {'ctx'}, dimensions={0}, use_global_device_ids=true | all-gather | bytes 860160 | tf_op jit(solution)/shard_map/all_gather | solution.py:692
  311.2 2.3 shard_map.254
  (322 shorter events, 84.2 us)
Async XLA Ops:
  11.1 16.6 %collective-permute-start.34 = (bf16[48,896]{1,0:T(8,128)(2,1)}, bf16[48,896]{1,0:T(8,128)(2,1)S(1)}, u32[]{:S(2)}, u32[]{:S(2)}) collective-permute-start(bf16[48,896]{1,0:T(8,128)(2,1)} %get-tuple-element.133), channel_id=1, source_target_pairs={{0,5},{1,4},{2,7},{3,6},{4,1},{5,0},{6,3},{7,2},{8,13},{9,12},{10,... | collective-permute-start | bytes 258056 | tf_op jit(solution)/shard_map/ppermute | solution.py:564
  13.4 17.1 %collective-permute-start.3 = (bf16[96,640]{1,0:T(8,128)(2,1)}, bf16[96,640]{1,0:T(8,128)(2,1)S(1)}, u32[]{:S(2)}, u32[]{:S(2)}) collective-permute-start(bf16[96,640]{1,0:T(8,128)(2,1)} %get-tuple-element.114.refs_0_), channel_id=1, source_target_pairs={{0,1},{1,0},{2,3},{3,2},{4,5},{5,4},{6,7},{7,6},{8,9},{9,8},{10,11... | collective-permute-start | bytes 368648 | tf_op jit(solution)/shard_map/ppermute | solution.py:564
  13.7 16.4 %collective-permute-start.35 = (bf16[48,896]{1,0:T(8,128)(2,1)}, bf16[48,896]{1,0:T(8,128)(2,1)S(1)}, u32[]{:S(2)}, u32[]{:S(2)}) collective-permute-start(bf16[48,896]{1,0:T(8,128)(2,1)} %get-tuple-element.134), channel_id=1, source_target_pairs={{0,6},{1,7},{2,4},{3,5},{4,2},{5,3},{6,0},{7,1},{8,14},{9,15},{10,... | collective-permute-start | bytes 258056 | tf_op jit(solution)/shard_map/ppermute | solution.py:564
  17.5 15.4 %collective-permute-start.2 = (bf16[96,640]{1,0:T(8,128)(2,1)}, bf16[96,640]{1,0:T(8,128)(2,1)S(1)}, u32[]{:S(2)}, u32[]{:S(2)}) collective-permute-start(bf16[96,640]{1,0:T(8,128)(2,1)} %get-tuple-element.114.refs_0_), channel_id=1, source_target_pairs={{0,6},{1,7},{2,4},{3,5},{4,2},{5,3},{6,0},{7,1},{8,14},{9,15},{10,... | collective-permute-start | bytes 368648 | tf_op jit(solution)/shard_map/ppermute | solution.py:564
  17.8 21.9 %collective-permute-start.1 = (bf16[96,640]{1,0:T(8,128)(2,1)}, bf16[96,640]{1,0:T(8,128)(2,1)S(1)}, u32[]{:S(2)}, u32[]{:S(2)}) collective-permute-start(bf16[96,640]{1,0:T(8,128)(2,1)} %get-tuple-element.114.refs_0_), channel_id=1, source_target_pairs={{0,4},{1,5},{2,6},{3,7},{4,0},{5,1},{6,2},{7,3},{8,12},{9,13},{10,... | collective-permute-start | bytes 368648 | tf_op jit(solution)/shard_map/ppermute | solution.py:564
  27.7 15.1 %collective-permute-start.15 = (bf16[96,832]{1,0:T(8,128)(2,1)}, bf16[96,832]{1,0:T(8,128)(2,1)S(1)}, u32[]{:S(2)}, u32[]{:S(2)}) collective-permute-start(bf16[96,832]{1,0:T(8,128)(2,1)} %get-tuple-element.117.refs_4_), channel_id=1, source_target_pairs={{0,6},{1,7},{2,4},{3,5},{4,2},{5,3},{6,0},{7,1},{8,14},{9,15},{10,... | collective-permute-start | bytes 479240 | tf_op jit(solution)/shard_map/ppermute | solution.py:564
  30.2 11.2 %collective-permute-start = (bf16[96,640]{1,0:T(8,128)(2,1)}, bf16[96,640]{1,0:T(8,128)(2,1)S(1)}, u32[]{:S(2)}, u32[]{:S(2)}) collective-permute-start(bf16[96,640]{1,0:T(8,128)(2,1)} %get-tuple-element.114.refs_0_), channel_id=1, source_target_pairs={{0,2},{1,3},{2,0},{3,1},{4,6},{5,7},{6,4},{7,5},{8,10},{9,11},{10,... | collective-permute-start | bytes 368648 | tf_op jit(solution)/shard_map/ppermute | solution.py:564
  30.5 19.8 %collective-permute-start.9 = (bf16[128,768]{1,0:T(8,128)(2,1)}, bf16[128,768]{1,0:T(8,128)(2,1)S(1)}, u32[]{:S(2)}, u32[]{:S(2)}) collective-permute-start(bf16[128,768]{1,0:T(8,128)(2,1)} %bitcast.18), channel_id=1, source_target_pairs={{0,24},{8,16},{16,8},{24,0},{1,25},{9,17},{17,9},{25,1},{2,26},{10... | collective-permute-start | bytes 589832 | tf_op jit(solution)/shard_map/ppermute | solution.py:564
  32.9 16.9 %collective-permute-start.14 = (bf16[96,832]{1,0:T(8,128)(2,1)}, bf16[96,832]{1,0:T(8,128)(2,1)S(1)}, u32[]{:S(2)}, u32[]{:S(2)}) collective-permute-start(bf16[96,832]{1,0:T(8,128)(2,1)} %get-tuple-element.117.refs_4_), channel_id=1, source_target_pairs={{0,4},{1,5},{2,6},{3,7},{4,0},{5,1},{6,2},{7,3},{8,12},{9,13},{10,... | collective-permute-start | bytes 479240 | tf_op jit(solution)/shard_map/ppermute | solution.py:564
  50.4 16.3 %collective-permute-start.16 = (bf16[96,832]{1,0:T(8,128)(2,1)}, bf16[96,832]{1,0:T(8,128)(2,1)S(1)}, u32[]{:S(2)}, u32[]{:S(2)}) collective-permute-start(bf16[96,832]{1,0:T(8,128)(2,1)} %get-tuple-element.117.refs_4_), channel_id=1, source_target_pairs={{0,1},{1,0},{2,3},{3,2},{4,5},{5,4},{6,7},{7,6},{8,9},{9,8},{10,11... | collective-permute-start | bytes 479240 | tf_op jit(solution)/shard_map/ppermute | solution.py:564
  50.8 13.4 %collective-permute-start.36 = (bf16[48,896]{1,0:T(8,128)(2,1)}, bf16[48,896]{1,0:T(8,128)(2,1)S(1)}, u32[]{:S(2)}, u32[]{:S(2)}) collective-permute-start(bf16[48,896]{1,0:T(8,128)(2,1)} %get-tuple-element.135), channel_id=1, source_target_pairs={{0,7},{1,6},{2,5},{3,4},{4,3},{5,2},{6,1},{7,0},{8,15},{9,14},{10,... | collective-permute-start | bytes 258056 | tf_op jit(solution)/shard_map/ppermute | solution.py:564
  53.3 14.0 %collective-permute-start.19 = (bf16[96,832]{1,0:T(8,128)(2,1)S(1)}, bf16[96,832]{1,0:T(8,128)(2,1)S(1)}, u32[]{:S(2)}, u32[]{:S(2)}) collective-permute-start(bf16[96,832]{1,0:T(8,128)(2,1)S(1)} %collective-permute-done.15.refs_7_), channel_id=1, source_target_pairs={{0,1},{1,0},{2,3},{3,2},{4,5},{5,4},{6,7},{7,6},{8,9},{9,8},{10,11... | collective-permute-start | bytes 479240 | tf_op jit(solution)/shard_map/ppermute | solution.py:564
  53.7 16.6 %collective-permute-start.18 = (bf16[96,832]{1,0:T(8,128)(2,1)S(1)}, bf16[96,832]{1,0:T(8,128)(2,1)S(1)}, u32[]{:S(2)}, u32[]{:S(2)}) collective-permute-start(bf16[96,832]{1,0:T(8,128)(2,1)S(1)} %collective-permute-done.14.refs_6_), channel_id=1, source_target_pairs={{0,1},{1,0},{2,3},{3,2},{4,5},{5,4},{6,7},{7,6},{8,9},{9,8},{10,11... | collective-permute-start | bytes 479240 | tf_op jit(solution)/shard_map/ppermute | solution.py:564
  53.8 19.0 %collective-permute-start.17 = (bf16[96,832]{1,0:T(8,128)(2,1)S(1)}, bf16[96,832]{1,0:T(8,128)(2,1)S(1)}, u32[]{:S(2)}, u32[]{:S(2)}) collective-permute-start(bf16[96,832]{1,0:T(8,128)(2,1)S(1)} %collective-permute-done.13.refs_5_), channel_id=1, source_target_pairs={{0,1},{1,0},{2,3},{3,2},{4,5},{5,4},{6,7},{7,6},{8,9},{9,8},{10,11... | collective-permute-start | bytes 479240 | tf_op jit(solution)/shard_map/ppermute | solution.py:564
  66.7 13.4 %collective-permute-start.11 = (bf16[512,192]{1,0:T(8,128)(2,1)}, bf16[512,192]{1,0:T(8,128)(2,1)S(1)}, u32[]{:S(2)}, u32[]{:S(2)}) collective-permute-start(bf16[512,192]{1,0:T(8,128)(2,1)} %get-tuple-element.116.refs_0_.refs_6_), channel_id=1, source_target_pairs={{0,16},{8,24},{16,0},{24,8},{1,17},{9,25},{17,1},{25,9},{2,18},{10... | collective-permute-start | bytes 589832 | tf_op jit(solution)/shard_map/ppermute | solution.py:564
  67.3 13.0 %collective-permute-start.10 = (bf16[512,192]{1,0:T(8,128)(2,1)}, bf16[512,192]{1,0:T(8,128)(2,1)S(1)}, u32[]{:S(2)}, u32[]{:S(2)}) collective-permute-start(bf16[512,192]{1,0:T(8,128)(2,1)} %get-tuple-element.116.refs_0_.refs_6_), channel_id=1, source_target_pairs={{0,8},{8,0},{16,24},{24,16},{1,9},{9,1},{17,25},{25,17},{2,10},{10... | collective-permute-start | bytes 589832 | tf_op jit(solution)/shard_map/ppermute | solution.py:564
  70.3 34.8 %collective-permute-start.39 = (bf16[192,896]{1,0:T(8,128)(2,1)}, bf16[192,896]{1,0:T(8,128)(2,1)S(1)}, u32[]{:S(2)}, u32[]{:S(2)}) collective-permute-start(bf16[192,896]{1,0:T(8,128)(2,1)} %get-tuple-element.136.refs_4_), channel_id=1, source_target_pairs={{0,24},{8,16},{16,8},{24,0},{1,25},{9,17},{17,9},{25,1},{2,26},{10... | collective-permute-start | bytes 1032200 | tf_op jit(solution)/shard_map/ppermute | solution.py:564
  72.8 33.7 %collective-permute-start.48 = (bf16[192,896]{1,0:T(8,128)(2,1)}, bf16[192,896]{1,0:T(8,128)(2,1)S(1)}, u32[]{:S(2)}, u32[]{:S(2)}) collective-permute-start(bf16[192,896]{1,0:T(8,128)(2,1)} %get-tuple-element.143.refs_4_), channel_id=1, source_target_pairs={{0,24},{8,16},{16,8},{24,0},{1,25},{9,17},{17,9},{25,1},{2,26},{10... | collective-permute-start | bytes 1032200 | tf_op jit(solution)/shard_map/ppermute | solution.py:564
  99.2 10.9 %collective-permute-start.46 = (bf16[192,896]{1,0:T(8,128)(2,1)S(1)}, bf16[192,896]{1,0:T(8,128)(2,1)S(1)}, u32[]{:S(2)}, u32[]{:S(2)}) collective-permute-start(bf16[192,896]{1,0:T(8,128)(2,1)S(1)} %copy-done.3), channel_id=1, source_target_pairs={{0,8},{8,0},{16,24},{24,16},{1,9},{9,1},{17,25},{25,17},{2,10},{10... | collective-permute-start | bytes 1032200 | tf_op jit(solution)/shard_map/ppermute | solution.py:564
  103.7 13.7 %collective-permute-start.45 = (bf16[192,768]{1,0:T(8,128)(2,1)}, bf16[192,768]{1,0:T(8,128)(2,1)S(1)}, u32[]{:S(2)}, u32[]{:S(2)}) collective-permute-start(bf16[192,768]{1,0:T(8,128)(2,1)} %get-tuple-element.142.refs_0_), channel_id=1, source_target_pairs={{0,24},{8,16},{16,8},{24,0},{1,25},{9,17},{17,9},{25,1},{2,26},{10... | collective-permute-start | bytes 884744 | tf_op jit(solution)/shard_map/ppermute | solution.py:564
  105.1 16.2 %collective-permute-start.44 = (bf16[192,768]{1,0:T(8,128)(2,1)}, bf16[192,768]{1,0:T(8,128)(2,1)S(1)}, u32[]{:S(2)}, u32[]{:S(2)}) collective-permute-start(bf16[192,768]{1,0:T(8,128)(2,1)} %get-tuple-element.142.refs_0_), channel_id=1, source_target_pairs={{0,16},{8,24},{16,0},{24,8},{1,17},{9,25},{17,1},{25,9},{2,18},{10... | collective-permute-start | bytes 884744 | tf_op jit(solution)/shard_map/ppermute | solution.py:564
  106.5 16.3 %collective-permute-start.43 = (bf16[192,768]{1,0:T(8,128)(2,1)}, bf16[192,768]{1,0:T(8,128)(2,1)S(1)}, u32[]{:S(2)}, u32[]{:S(2)}) collective-permute-start(bf16[192,768]{1,0:T(8,128)(2,1)} %get-tuple-element.142.refs_0_), channel_id=1, source_target_pairs={{0,8},{8,0},{16,24},{24,16},{1,9},{9,1},{17,25},{25,17},{2,10},{10... | collective-permute-start | bytes 884744 | tf_op jit(solution)/shard_map/ppermute | solution.py:564
  107.2 29.3 %collective-permute-start.38 = (bf16[192,896]{1,0:T(8,128)(2,1)S(1)}, bf16[192,896]{1,0:T(8,128)(2,1)S(1)}, u32[]{:S(2)}, u32[]{:S(2)}) collective-permute-start(bf16[192,896]{1,0:T(8,128)(2,1)S(1)} %copy-done.1), channel_id=1, source_target_pairs={{0,16},{8,24},{16,0},{24,8},{1,17},{9,25},{17,1},{25,9},{2,18},{10... | collective-permute-start | bytes 1032200 | tf_op jit(solution)/shard_map/ppermute | solution.py:564
  110.1 27.2 %collective-permute-start.37 = (bf16[192,896]{1,0:T(8,128)(2,1)S(1)}, bf16[192,896]{1,0:T(8,128)(2,1)S(1)}, u32[]{:S(2)}, u32[]{:S(2)}) collective-permute-start(bf16[192,896]{1,0:T(8,128)(2,1)S(1)} %copy-done.1), channel_id=1, source_target_pairs={{0,8},{8,0},{16,24},{24,16},{1,9},{9,1},{17,25},{25,17},{2,10},{10... | collective-permute-start | bytes 1032200 | tf_op jit(solution)/shard_map/ppermute | solution.py:564
  117.4 21.2 %collective-permute-start.29 = (bf16[192,768]{1,0:T(8,128)(2,1)}, bf16[192,768]{1,0:T(8,128)(2,1)S(1)}, u32[]{:S(2)}, u32[]{:S(2)}) collective-permute-start(bf16[192,768]{1,0:T(8,128)(2,1)} %get-tuple-element.127.refs_0_), channel_id=1, source_target_pairs={{0,24},{8,16},{16,8},{24,0},{1,25},{9,17},{17,9},{25,1},{2,26},{10... | collective-permute-start | bytes 884744 | tf_op jit(solution)/shard_map/ppermute | solution.py:564
  121.3 20.0 %collective-permute-start.28 = (bf16[192,768]{1,0:T(8,128)(2,1)}, bf16[192,768]{1,0:T(8,128)(2,1)S(1)}, u32[]{:S(2)}, u32[]{:S(2)}) collective-permute-start(bf16[192,768]{1,0:T(8,128)(2,1)} %get-tuple-element.127.refs_0_), channel_id=1, source_target_pairs={{0,16},{8,24},{16,0},{24,8},{1,17},{9,25},{17,1},{25,9},{2,18},{10... | collective-permute-start | bytes 884744 | tf_op jit(solution)/shard_map/ppermute | solution.py:564
  122.8 20.1 %collective-permute-start.27 = (bf16[192,768]{1,0:T(8,128)(2,1)}, bf16[192,768]{1,0:T(8,128)(2,1)S(1)}, u32[]{:S(2)}, u32[]{:S(2)}) collective-permute-start(bf16[192,768]{1,0:T(8,128)(2,1)} %get-tuple-element.127.refs_0_), channel_id=1, source_target_pairs={{0,8},{8,0},{16,24},{24,16},{1,9},{9,1},{17,25},{25,17},{2,10},{10... | collective-permute-start | bytes 884744 | tf_op jit(solution)/shard_map/ppermute | solution.py:564
  136.5 21.3 %collective-permute-start.62 = (bf16[192,768]{1,0:T(8,128)(2,1)}, bf16[192,768]{1,0:T(8,128)(2,1)S(1)}, u32[]{:S(2)}, u32[]{:S(2)}) collective-permute-start(bf16[192,768]{1,0:T(8,128)(2,1)} %get-tuple-element.161), channel_id=1, source_target_pairs={{0,8},{8,0},{16,24},{24,16},{1,9},{9,1},{17,25},{25,17},{2,10},{10... | collective-permute-start | bytes 884744 | tf_op jit(solution)/shard_map/ppermute | solution.py:564
  137.3 22.1 %collective-permute-start.63 = (bf16[192,768]{1,0:T(8,128)(2,1)}, bf16[192,768]{1,0:T(8,128)(2,1)S(1)}, u32[]{:S(2)}, u32[]{:S(2)}) collective-permute-start(bf16[192,768]{1,0:T(8,128)(2,1)} %get-tuple-element.162), channel_id=1, source_target_pairs={{0,16},{8,24},{16,0},{24,8},{1,17},{9,25},{17,1},{25,9},{2,18},{10... | collective-permute-start | bytes 884744 | tf_op jit(solution)/shard_map/ppermute | solution.py:564
  138.6 20.8 %collective-permute-start.64 = (bf16[192,768]{1,0:T(8,128)(2,1)}, bf16[192,768]{1,0:T(8,128)(2,1)S(1)}, u32[]{:S(2)}, u32[]{:S(2)}) collective-permute-start(bf16[192,768]{1,0:T(8,128)(2,1)} %get-tuple-element.163), channel_id=1, source_target_pairs={{0,24},{8,16},{16,8},{24,0},{1,25},{9,17},{17,9},{25,1},{2,26},{10... | collective-permute-start | bytes 884744 | tf_op jit(solution)/shard_map/ppermute | solution.py:564
  157.4 12.7 %collective-permute-start.60 = (bf16[192,768]{1,0:T(8,128)(2,1)}, bf16[192,768]{1,0:T(8,128)(2,1)S(1)}, u32[]{:S(2)}, u32[]{:S(2)}) collective-permute-start(bf16[192,768]{1,0:T(8,128)(2,1)} %get-tuple-element.158), channel_id=1, source_target_pairs={{0,16},{8,24},{16,0},{24,8},{1,17},{9,25},{17,1},{25,9},{2,18},{10... | collective-permute-start | bytes 884744 | tf_op jit(solution)/shard_map/ppermute | solution.py:564
  157.9 12.2 %collective-permute-start.61 = (bf16[192,768]{1,0:T(8,128)(2,1)}, bf16[192,768]{1,0:T(8,128)(2,1)S(1)}, u32[]{:S(2)}, u32[]{:S(2)}) collective-permute-start(bf16[192,768]{1,0:T(8,128)(2,1)} %get-tuple-element.159), channel_id=1, source_target_pairs={{0,24},{8,16},{16,8},{24,0},{1,25},{9,17},{17,9},{25,1},{2,26},{10... | collective-permute-start | bytes 884744 | tf_op jit(solution)/shard_map/ppermute | solution.py:564
  180.2 11.7 %collective-permute-start.69 = (bf16[48,768]{1,0:T(8,128)(2,1)}, bf16[48,768]{1,0:T(8,128)(2,1)S(1)}, u32[]{:S(2)}, u32[]{:S(2)}) collective-permute-start(bf16[48,768]{1,0:T(8,128)(2,1)} %get-tuple-element.169), channel_id=1, source_target_pairs={{0,5},{1,4},{2,7},{3,6},{4,1},{5,0},{6,3},{7,2},{8,13},{9,12},{10,... | collective-permute-start | bytes 221192 | tf_op jit(solution)/shard_map/ppermute | solution.py:564
  180.4 11.5 %collective-permute-start.70 = (bf16[48,768]{1,0:T(8,128)(2,1)}, bf16[48,768]{1,0:T(8,128)(2,1)S(1)}, u32[]{:S(2)}, u32[]{:S(2)}) collective-permute-start(bf16[48,768]{1,0:T(8,128)(2,1)} %get-tuple-element.170), channel_id=1, source_target_pairs={{0,6},{1,7},{2,4},{3,5},{4,2},{5,3},{6,0},{7,1},{8,14},{9,15},{10,... | collective-permute-start | bytes 221192 | tf_op jit(solution)/shard_map/ppermute | solution.py:564
  199.2 24.2 %collective-permute-start.49 = (bf16[192,768]{1,0:T(8,128)(2,1)S(1)}, bf16[192,768]{1,0:T(8,128)(2,1)S(1)}, u32[]{:S(2)}, u32[]{:S(2)}) collective-permute-start(bf16[192,768]{1,0:T(8,128)(2,1)S(1)} %copy-done.73), channel_id=1, source_target_pairs={{0,8},{8,0},{16,24},{24,16},{1,9},{9,1},{17,25},{25,17},{2,10},{10... | collective-permute-start | bytes 884744 | tf_op jit(solution)/shard_map/ppermute | solution.py:564
  200.5 23.8 %collective-permute-start.50 = (bf16[192,768]{1,0:T(8,128)(2,1)S(1)}, bf16[192,768]{1,0:T(8,128)(2,1)S(1)}, u32[]{:S(2)}, u32[]{:S(2)}) collective-permute-start(bf16[192,768]{1,0:T(8,128)(2,1)S(1)} %copy-done.72), channel_id=1, source_target_pairs={{0,16},{8,24},{16,0},{24,8},{1,17},{9,25},{17,1},{25,9},{2,18},{10... | collective-permute-start | bytes 884744 | tf_op jit(solution)/shard_map/ppermute | solution.py:564
  220.5 43.2 %collective-permute-start.78 = (bf16[384,896]{1,0:T(8,128)(2,1)}, bf16[384,896]{1,0:T(8,128)(2,1)S(1)}, u32[]{:S(2)}, u32[]{:S(2)}) collective-permute-start(bf16[384,896]{1,0:T(8,128)(2,1)} %get-tuple-element.191), channel_id=1, source_target_pairs={{0,1},{1,0},{2,3},{3,2},{4,5},{5,4},{6,7},{7,6},{8,9},{9,8},{10,11... | collective-permute-start | bytes 2064392 | tf_op jit(solution)/shard_map/ppermute | solution.py:564
  222.6 15.0 %collective-permute-start.40 = (bf16[192,768]{1,0:T(8,128)(2,1)}, bf16[192,768]{1,0:T(8,128)(2,1)S(1)}, u32[]{:S(2)}, u32[]{:S(2)}) collective-permute-start(bf16[192,768]{1,0:T(8,128)(2,1)} %get-tuple-element.139), channel_id=1, source_target_pairs={{0,8},{8,0},{16,24},{24,16},{1,9},{9,1},{17,25},{25,17},{2,10},{10... | collective-permute-start | bytes 884744 | tf_op jit(solution)/shard_map/ppermute | solution.py:564
  223.4 14.3 %collective-permute-start.41 = (bf16[192,768]{1,0:T(8,128)(2,1)S(1)}, bf16[192,768]{1,0:T(8,128)(2,1)S(1)}, u32[]{:S(2)}, u32[]{:S(2)}) collective-permute-start(bf16[192,768]{1,0:T(8,128)(2,1)S(1)} %copy-done.75), channel_id=1, source_target_pairs={{0,16},{8,24},{16,0},{24,8},{1,17},{9,25},{17,1},{25,9},{2,18},{10... | collective-permute-start | bytes 884744 | tf_op jit(solution)/shard_map/ppermute | solution.py:564
  224.2 19.4 %collective-permute-start.42 = (bf16[192,768]{1,0:T(8,128)(2,1)S(1)}, bf16[192,768]{1,0:T(8,128)(2,1)S(1)}, u32[]{:S(2)}, u32[]{:S(2)}) collective-permute-start(bf16[192,768]{1,0:T(8,128)(2,1)S(1)} %copy-done.74), channel_id=1, source_target_pairs={{0,24},{8,16},{16,8},{24,0},{1,25},{9,17},{17,9},{25,1},{2,26},{10... | collective-permute-start | bytes 884744 | tf_op jit(solution)/shard_map/ppermute | solution.py:564
  254.1 24.0 %collective-permute-start.75 = (bf16[128,768]{1,0:T(8,128)(2,1)S(1)}, bf16[128,768]{1,0:T(8,128)(2,1)S(1)}, u32[]{:S(2)}, u32[]{:S(2)}) collective-permute-start(bf16[128,768]{1,0:T(8,128)(2,1)S(1)} %copy-done.78), channel_id=1, source_target_pairs={{0,8},{8,0},{16,24},{24,16},{1,9},{9,1},{17,25},{25,17},{2,10},{10... | collective-permute-start | bytes 589832 | tf_op jit(solution)/shard_map/ppermute | solution.py:564
  257.0 20.6 %collective-permute-start.57 = (bf16[48,768]{1,0:T(8,128)(2,1)}, bf16[48,768]{1,0:T(8,128)(2,1)S(1)}, u32[]{:S(2)}, u32[]{:S(2)}) collective-permute-start(bf16[48,768]{1,0:T(8,128)(2,1)} %get-tuple-element.154), channel_id=1, source_target_pairs={{0,6},{1,7},{2,4},{3,5},{4,2},{5,3},{6,0},{7,1},{8,14},{9,15},{10,... | collective-permute-start | bytes 221192 | tf_op jit(solution)/shard_map/ppermute | solution.py:564
  259.5 18.3 %collective-permute-start.58 = (bf16[48,768]{1,0:T(8,128)(2,1)}, bf16[48,768]{1,0:T(8,128)(2,1)S(1)}, u32[]{:S(2)}, u32[]{:S(2)}) collective-permute-start(bf16[48,768]{1,0:T(8,128)(2,1)} %get-tuple-element.155), channel_id=1, source_target_pairs={{0,7},{1,6},{2,5},{3,4},{4,3},{5,2},{6,1},{7,0},{8,15},{9,14},{10,... | collective-permute-start | bytes 221192 | tf_op jit(solution)/shard_map/ppermute | solution.py:564
  263.7 30.2 %collective-permute-start.76 = (bf16[128,768]{1,0:T(8,128)(2,1)S(1)}, bf16[128,768]{1,0:T(8,128)(2,1)S(1)}, u32[]{:S(2)}, u32[]{:S(2)}) collective-permute-start(bf16[128,768]{1,0:T(8,128)(2,1)S(1)} %copy-done.77), channel_id=1, source_target_pairs={{0,16},{8,24},{16,0},{24,8},{1,17},{9,25},{17,1},{25,9},{2,18},{10... | collective-permute-start | bytes 589832 | tf_op jit(solution)/shard_map/ppermute | solution.py:564
  263.8 30.2 %collective-permute-start.77 = (bf16[128,768]{1,0:T(8,128)(2,1)S(1)}, bf16[128,768]{1,0:T(8,128)(2,1)S(1)}, u32[]{:S(2)}, u32[]{:S(2)}) collective-permute-start(bf16[128,768]{1,0:T(8,128)(2,1)S(1)} %copy-done.76), channel_id=1, source_target_pairs={{0,24},{8,16},{16,8},{24,0},{1,25},{9,17},{17,9},{25,1},{2,26},{10... | collective-permute-start | bytes 589832 | tf_op jit(solution)/shard_map/ppermute | solution.py:564
  277.7 19.4 %collective-permute-start.79 = (bf16[96,896]{1,0:T(8,128)(2,1)}, bf16[96,896]{1,0:T(8,128)(2,1)S(1)}, u32[]{:S(2)}, u32[]{:S(2)}) collective-permute-start(bf16[96,896]{1,0:T(8,128)(2,1)} %get-tuple-element.193), channel_id=1, source_target_pairs={{0,2},{1,3},{2,0},{3,1},{4,6},{5,7},{6,4},{7,5},{8,10},{9,11},{10,... | collective-permute-start | bytes 516104 | tf_op jit(solution)/shard_map/ppermute | solution.py:564
  277.7 19.3 %collective-permute-start.80 = (bf16[96,896]{1,0:T(8,128)(2,1)}, bf16[96,896]{1,0:T(8,128)(2,1)S(1)}, u32[]{:S(2)}, u32[]{:S(2)}) collective-permute-start(bf16[96,896]{1,0:T(8,128)(2,1)} %get-tuple-element.194), channel_id=1, source_target_pairs={{0,4},{1,5},{2,6},{3,7},{4,0},{5,1},{6,2},{7,3},{8,12},{9,13},{10,... | collective-permute-start | bytes 516104 | tf_op jit(solution)/shard_map/ppermute | solution.py:564
  278.2 18.9 %collective-permute-start.81 = (bf16[96,896]{1,0:T(8,128)(2,1)}, bf16[96,896]{1,0:T(8,128)(2,1)S(1)}, u32[]{:S(2)}, u32[]{:S(2)}) collective-permute-start(bf16[96,896]{1,0:T(8,128)(2,1)} %get-tuple-element.195), channel_id=1, source_target_pairs={{0,6},{1,7},{2,4},{3,5},{4,2},{5,3},{6,0},{7,1},{8,14},{9,15},{10,... | collective-permute-start | bytes 516104 | tf_op jit(solution)/shard_map/ppermute | solution.py:564
  (126 other events, 1342.1 us)
where the time goes:
time: 314 us; the launch traced here: 313 us
  starting transfers between devices  100 us (32%)
  Pallas kernels  97.6 us (31%)
  waiting for transfers between devices  94.3 us (30%)
  blocking collectives  11.4 us (4%)
  local copies, waits for them, and re-layouts  8.09 us (3%)
    ppermute x82, starting transfers between devices, permute(): return lax.ppermute(x, axis, [(i, i ^ k) for i in range(n)])  100 us
    ppermute x82, waiting for transfers between devices, permute(): return lax.ppermute(x, axis, [(i, i ^ k) for i in range(n)])  94.3 us
    pallas_call x15, Pallas kernels, call(): pl.pallas_call(kernel, out_shape=[jax.ShapeDtypeStruct(s, d) for s, d in...  55.6 us
    pallas_call x2, Pallas kernels, experts(): pl.pallas_call(functools.partial(expert_kernel, cfg, first), grid=(steps,...  24.4 us
    pallas_call x2, Pallas kernels, expert_weights(): pl.pallas_call(expert_weights_kernel, grid=(steps,), out_shape=[jax.Shape...  17.7 us
    all_gather x1, blocking collectives, body(): everyone = lax.all_gather(total, 'ctx', axis=0, tiled=True)  11.4 us
    unnamed x185, local copies, waits for them, and re-layouts  8.09 us
  transfers between devices with their start and end apart: 82, of which 30 were waited for; matrix products, arithmetic and copies ran while one was open for 0% of the time, Pallas kernels for 27%

commit v1 on v0

--- a/solution.py
+++ b/solution.py
@@ -228,17 +228,19 @@
         outs[k][...] = b16(dot(b16(hot), hidden, TN))
 
 
-def arrange(cfg, order_ref, *refs):
+def arrange(cfg, cuts, order_ref, *refs):
     pieces, outs = refs[: cfg.NE], refs[cfg.NE :]
     rows = jnp.concatenate([p[...] for p in pieces], axis=0)
     total = rows.shape[0]
     part = total // HALVES
-    for n, out in enumerate(outs):
+    for n in range(HALVES):
         hot = (iota((part, total), 0) + n * part == order_ref[...]).astype(jnp.float32)
-        out[...] = b16(dot(b16(hot), rows))
-
-
-def gather_sum(cfg, order_ref, *refs):
+        half = b16(dot(b16(hot), rows))
+        for m, (lo, hi) in enumerate(cuts):
+            outs[n * len(cuts) + m][...] = half[:, lo:hi]
+
+
+def gather_sum(cfg, idx_ref, order_ref, *refs):
     ins, outs = refs[: HALVES * cfg.NC], refs[HALVES * cfg.NC :]
     halves = []
     for n in range(HALVES):
@@ -249,8 +251,14 @@
         halves.append(b16(total))
     rows = jnp.concatenate(halves, axis=0)
     count = rows.shape[0]
-    hot = (iota((count, count), 0) == order_ref[...]).astype(jnp.float32)
+    place = order_ref[0:1]
+    if len(outs) == 1:
+        place = order_ref[1:2] + (order_ref[2:3] ^ idx_ref[1]) * CAP
+    hot = (iota((count, count), 0) == place).astype(jnp.float32)
     back = b16(dot(b16(hot), rows, TN))
+    if len(outs) == 1:
+        outs[0][...] = back
+        return
     for k, out in enumerate(outs):
         out[...] = back[k * cfg.XC : (k + 1) * cfg.XC]
 
@@ -258,6 +266,9 @@
 def collect(cfg, idx_ref, ids, pieces):
     slot_a, slot_b = slots_of(ids, cfg.E)
     total = None
+    if len(pieces) == 1:
+        hot = hot_slots(slot_a, 0, cfg.E * CAP) + hot_slots(slot_b, 0, cfg.E * CAP)
+        return dot(b16(hot), pieces[0][...])
     for k, piece in enumerate(pieces):
         start = (idx_ref[1] ^ k) * cfg.XC
         hot = hot_slots(slot_a, start, cfg.XC) + hot_slots(slot_b, start, cfg.XC)
@@ -283,17 +294,27 @@
     half_ref[...] = b16(grad_mixed)
 
 
-def expert_kernel(cfg, first, idx_ref, *refs):
+def joined(refs):
+    return jnp.concatenate([r[...] for r in refs], axis=0)
+
+
+def join_parts(refs, parts):
+    rows = [jnp.concatenate([r[...] for r in refs[n : n + parts]], axis=1) for n in range(0, len(refs), parts)]
+    return jnp.concatenate(rows, axis=0)
+
+
+def expert_kernel(cfg, first, parts, idx_ref, *refs):
     NC, D, E = cfg.NC, cfg.D, cfg.E
-    rows_in, ups_in = refs[:NC], refs[NC : 2 * NC]
-    win_ref, wout_ref, router_ref = refs[2 * NC : 2 * NC + 3]
-    outs = refs[2 * NC + 3 :]
+    rows_in, refs = refs[:NC], refs[NC:]
+    ups_in, refs = refs[: parts * NC], refs[parts * NC :]
+    win_ref, wout_ref, router_ref = refs[:3]
+    outs = refs[3:]
     back, fwd = outs[:NC], outs[NC : 2 * NC]
     rows_out, up_out, act_out, pre_out, route_out = outs[2 * NC :]
     step = pl.program_id(0)
     own = idx_ref[1] * cfg.X + first + step
-    rows = jnp.concatenate([r[...] for r in rows_in], axis=0)
-    ups = jnp.concatenate([u[...] for u in ups_in], axis=0)
+    rows = joined(rows_in)
+    ups = join_parts(ups_in, parts)
     count = rows.shape[0]
     win, wout = win_ref[0], wout_ref[0]
     other = ups[:, D : D + 1].astype(jnp.float32).astype(jnp.int32)
@@ -342,7 +363,7 @@
     pre_out[0] = grad_pre
 
 
-def experts(cfg, half, idx, rows, ups, w_in, w_out, router):
+def experts(cfg, half, cuts, idx, rows, ups, w_in, w_out, router):
     NC, D, FL = cfg.NC, cfg.D, w_in.shape[2]
     steps = cfg.X // HALVES
     first = half * steps
@@ -354,12 +375,12 @@
     here = lambda a, b: pl.BlockSpec((1, a, b), lambda s: (s, 0, 0))
     saved = [((steps, count, w), jnp.bfloat16) for w in (D, D, FL, FL)]
     outs = [((steps * each, D), jnp.bfloat16)] * (2 * NC) + saved + [((D, 2 * cfg.E), jnp.float32)]
-    in_specs = [SMEM] + [row(D)] * NC + [row(D + EXTRA)] * NC
+    in_specs = [SMEM] + [row(D)] * NC + [row(hi - lo) for lo, hi in cuts] * NC
     in_specs += [per(D, FL), per(FL, D), fixed((D, cfg.E))]
     out_specs = [row(D)] * (2 * NC) + [here(count, w) for w in (D, D, FL, FL)]
     out_specs += [fixed((D, 2 * cfg.E))]
     return pl.pallas_call(
-        functools.partial(expert_kernel, cfg, first),
+        functools.partial(expert_kernel, cfg, first, len(cuts)),
         grid=(steps,),
         out_shape=[jax.ShapeDtypeStruct(s, d) for s, d in outs],
         in_specs=in_specs,
@@ -534,9 +555,12 @@
     out_ref[...] = mix_ref[...] + moved
 
 
-def last_weights(cfg, all_ref, q_ref, k_ref, v_ref, o_ref, router_ref, one_ref, two_ref, table_ref):
+def last_weights(cfg, idx_ref, *refs):
+    ins, (q_ref, k_ref, v_ref, o_ref, router_ref, one_ref, two_ref, table_ref, all_ref) = refs[: cfg.NC], refs[cfg.NC :]
     R, CQ, CO, D, hl, E = cfg.rows, cfg.CQ, cfg.CO, cfg.D, cfg.hl, cfg.E
-    pieces = [f32(all_ref[n * R : (n + 1) * R, :]) for n in range(cfg.NC)]
+    for k, piece in enumerate(ins):
+        all_ref[idx_ref[0] ^ k] = f32(piece[...])
+    pieces = [all_ref[n] for n in range(cfg.NC)]
     for t, ref in enumerate((q_ref, k_ref, v_ref)):
         full = jnp.concatenate([p[:, t * CQ : (t + 1) * CQ] for p in pieces], axis=1)
         ref[...] = full[:, :D]
@@ -566,6 +590,15 @@
 
 def spread(first, rest, axis, n):
     return [first] + [permute(x, axis, k, n) for k, x in zip(range(1, n), rest, strict=True)]
+
+
+def two_steps(parts):
+    got = []
+    for part, (near, via) in zip(parts, ((1, 2), (2, 1)), strict=True):
+        one, two = permute(part, "ctx", near, 4), permute(part, "ctx", via, 4)
+        far = permute(one, "ctx", via, 4)
+        got.append([part, one, two, far] if near == 1 else [part, two, one, far])
+    return got
 
 
 def gather_rows(cfg, x):
@@ -617,24 +650,41 @@
     ks = np.arange(E * CAP)
     to = (ks % cfg.XC) // CAP * (NE * CAP) + ks // cfg.XC * CAP + ks % CAP
     order = jnp.asarray(to.reshape(1, -1), jnp.int32)
-
-    def to_experts(sent):
+    source = ks // cfg.XC
+    orders = jnp.asarray(np.stack([to, to - source * CAP, source]), jnp.int32)
+
+    def to_experts(sent, cuts):
         got = spread(sent[0], sent[1:], "ep", NE)
-        w = sent[0].shape[1]
-        halves = call(
-            functools.partial(arrange, cfg), [order, *got], [((E * CAP // HALVES, w), bf)] * HALVES,
-            n_smem=0,
+        parts = call(
+            functools.partial(arrange, cfg, cuts), [order, *got],
+            [((E * CAP // HALVES, hi - lo), bf) for lo, hi in cuts] * HALVES, n_smem=0,
         )
-        return [spread(h, [h] * (NC - 1), "ctx", NC) for h in halves]
-
-    def from_experts(parts):
+        out = []
+        for n in range(HALVES):
+            here = parts[n * len(cuts) : (n + 1) * len(cuts)]
+            if len(cuts) == 2 and NC == 4:
+                got = two_steps(here)
+            else:
+                got = [spread(h, [h] * (NC - 1), "ctx", NC) for h in here]
+            out.append([piece[k] for k in range(NC) for piece in got])
+        return out
+
+    def from_experts(parts, whole):
         got = []
         for half in parts:
             got += spread(half[0], half[1:], "ctx", NC)
-        sent = call(functools.partial(gather_sum, cfg), [order, *got], [((cfg.XC, D), bf)] * NE, n_smem=0)
+        sent = call(
+            functools.partial(gather_sum, cfg), [idx, orders, *got],
+            [((E * CAP, D), bf)] if whole else [((cfg.XC, D), bf)] * NE,
+        )
+        if whole:
+            return [lax.all_to_all(sent[0], "ep", split_axis=0, concat_axis=0, tiled=True)]
         return spread(sent[0], sent[1:], "ep", NE)
 
-    ups = to_experts(up_send)
+    W2 = D + EXTRA
+    cut = (D // 2 + EXTRA - 1) // EXTRA * EXTRA
+    cuts = ((0, cut), (cut, W2))
+    ups = to_experts(up_send, cuts)
     nb = S // TILE
     x_all, q, k, v, hidden, att, lse, bias, w_all, gains = call(
         functools.partial(attn_forward, cfg), [idx, bucket, *first, *x_pieces],
@@ -648,21 +698,21 @@
         [((B, D), fl), ((NC * CQ, D), bf), ((D, E), bf)] + [((cfg.XC, D), bf)] * NE,
         scratch=[pltpu.VMEM((D, D + E), bf)],
     )
-    rows = to_experts(sent)
+    rows = to_experts(sent, ((0, D),))
     backs, fwds, routes, grads = [], [], [], []
     for half in range(HALVES):
-        got = experts(cfg, half, idx, rows[half], ups[half], expert_in, expert_out, router)
+        got = experts(cfg, half, cuts, idx, rows[half], ups[half], expert_in, expert_out, router)
         backs.append(got[:NC])
         fwds.append(got[NC : 2 * NC])
         grads = expert_weights(cfg, half, *got[2 * NC : 2 * NC + 4], grads)
         routes.append(got[-1])
     grad_expert_in, grad_expert_out = grads
-    back = from_experts(backs)
+    back = from_experts(backs, False)
     mix, mix_half, gg = call(
         functools.partial(moe_back, cfg), [idx, ids, mixed, gains, up_own, *back],
         [((B, D), fl), ((B, D), bf), ((8, D), fl)],
     )
-    fwd = from_experts(fwds)
+    fwd = from_experts(fwds, True)
     (block_output,) = call(functools.partial(finish_forward, cfg), [idx, ids, mixed, *fwd], [((B, D), fl)])
     gm = spread(mix_half, [mix_half] * (NC - 1), "ctx", NC)
     WC = 3 * CQ + CO + EXTRA
@@ -689,12 +739,13 @@
     pairs = call(functools.partial(add_pairs, cfg), [mine, theirs], [((R, WC), bf)] * (NE // 2), n_smem=0)
     pairs = [pairs[0]] + [permute(pairs[j], "ep", 2 * j, NE) for j in range(1, NE // 2)]
     (total,) = call(add_all, pairs, [((R, WC), bf)], n_smem=0)
-    everyone = lax.all_gather(total, "ctx", axis=0, tiled=True)
+    everyone = spread(total, [total] * (NC - 1), "ctx", NC)
     (input_grad,) = call(last_input, [x_own, gains, mix, *gh], [((B, D), fl)], n_smem=0)
     nbl = bias_table.shape[0]
     gq, gk, gv, go, grouter, gone, gtwo, gtable = call(
-        functools.partial(last_weights, cfg), [everyone],
-        [((R, D), fl)] * 4 + [((E, R), fl), ((1, R), fl), ((1, R), fl), ((nbl, cfg.H), fl)], n_smem=0,
+        functools.partial(last_weights, cfg), [idx, *everyone],
+        [((R, D), fl)] * 4 + [((E, R), fl), ((1, R), fl), ((1, R), fl), ((nbl, cfg.H), fl)],
+        scratch=[pltpu.VMEM((NC, R, WC), fl)],
     )
     return (
         block_output[None], input_grad[None], gq, gk, gv, go, grouter.T, gone[0], gtwo[0], gtable,

time: 314 us -> 305 us (0.971)
  blocking collectives: 11.4 us -> 0 us
  waiting for transfers between devices: 94.3 us -> 87.1 us
  starting transfers between devices: 100 us -> 105 us
  local copies, waits for them, and re-layouts: 8.09 us -> 11.6 us
    all_gather x1 -> x0, blocking collectives: 11.4 us -> none  [body(): everyone = lax.all_gather(total, 'ctx', axis=0, tiled=True)]
    ppermute x82 -> x84, waiting for transfers between devices: 94.3 us -> 87.1 us  [permute(): return lax.ppermute(x, axis, [(i, i ^ k) for i in range(n)])]
    all_to_all x0 -> x1, starting transfers between devices: none -> 5.4 us  [from_experts(): lax.all_to_all(sent[0], 'ep', split_axis=0, concat_axis=0, tiled=True)]
    unnamed x185 -> x193, local copies, waits for them, and re-layouts: 8.09 us -> 11.6 us
    ppermute x82 -> x84, starting transfers between devices: 100 us -> 99.6 us  [permute(): return lax.ppermute(x, axis, [(i, i ^ k) for i in range(n)])]
  transfers between devices with their start and end apart: 82 -> 85, of which waited for: 30 -> 20; matrix products, arithmetic and copies ran while one was open for 0% -> 0% of each run, Pallas kernels for 27% -> 29%
where the time goes in v1:
time: 305 us; the launch traced here: 303 us
  starting transfers between devices  105 us (34%)
  Pallas kernels  97.4 us (32%)
  waiting for transfers between devices  87.1 us (29%)
  local copies, waits for them, and re-layouts  11.6 us (4%)
    ppermute x84, starting transfers between devices, permute(): return lax.ppermute(x, axis, [(i, i ^ k) for i in range(n)])  99.6 us
    ppermute x84, waiting for transfers between devices, permute(): return lax.ppermute(x, axis, [(i, i ^ k) for i in range(n)])  87.1 us
    pallas_call x15, Pallas kernels, call(): pl.pallas_call(kernel, out_shape=[jax.ShapeDtypeStruct(s, d) for s, d in...  55.6 us
    pallas_call x2, Pallas kernels, experts(): pl.pallas_call(functools.partial(expert_kernel, cfg, first, len(cuts)), g...  24.2 us
    pallas_call x2, Pallas kernels, expert_weights(): pl.pallas_call(expert_weights_kernel, grid=(steps,), out_shape=[jax.Shape...  17.6 us
    unnamed x193, local copies, waits for them, and re-layouts  11.6 us
  transfers between devices with their start and end apart: 85, of which 20 were waited for; matrix products, arithmetic and copies ran while one was open for 0% of the time, Pallas kernels for 29%

profile of v1, /device:TPU:0, one launch (start us, length us, event | category | flops | bytes accessed | tf_op | source)
XLA Modules:
  0.0 303.2 jit_solution(10579409942098020232)
XLA Ops:
  2.7 2.5 shard_map.251
  5.7 2.6 collective-permute-start.31
  8.4 2.2 shard_map.247
  10.8 3.0 collective-permute-start.33
  13.8 3.4 %collective-permute-start.2 = (bf16[96,640]{1,0:T(8,128)(2,1)}, bf16[96,640]{1,0:T(8,128)(2,1)S(1)}, u32[]{:S(2)}, u32[]{:S(2)}) collective-permute-start(bf16[96,640]{1,0:T(8,128)(2,1)} %get-tuple-element.108.refs_0_), channel_id=1, source_target_pairs={{0,6},{1,7},{2,4},{3,5},{4,2},{5,3},{6,0},{7,1},{8,14},{9,15},{10,... | collective-permute-start | bytes 368648 | tf_op jit(solution)/shard_map/ppermute | solution.py:588
  17.6 7.8 %collective-permute-done.33.refs_4_ = bf16[48,896]{1,0:T(8,128)(2,1)S(1)} collective-permute-done((bf16[48,896]{1,0:T(8,128)(2,1)}, bf16[48,896]{1,0:T(8,128)(2,1)S(1)}, u32[]{:S(2)}, u32[]{:S(2)}) %collective-permute-start.33) | collective-permute-done | bytes 86048 | tf_op jit(solution)/shard_map/ppermute | solution.py:588
  26.3 4.2 %collective-permute-start = (bf16[96,640]{1,0:T(8,128)(2,1)}, bf16[96,640]{1,0:T(8,128)(2,1)S(1)}, u32[]{:S(2)}, u32[]{:S(2)}) collective-permute-start(bf16[96,640]{1,0:T(8,128)(2,1)} %get-tuple-element.108.refs_0_), channel_id=1, source_target_pairs={{0,2},{1,3},{2,0},{3,1},{4,6},{5,7},{6,4},{7,5},{8,10},{9,11},{10,... | collective-permute-start | bytes 368648 | tf_op jit(solution)/shard_map/ppermute | solution.py:588
  30.5 2.4 collective-permute-start.9
  32.9 2.5 collective-permute-start.15
  35.5 3.7 %collective-permute-start.14 = (bf16[96,832]{1,0:T(8,128)(2,1)}, bf16[96,832]{1,0:T(8,128)(2,1)S(1)}, u32[]{:S(2)}, u32[]{:S(2)}) collective-permute-start(bf16[96,832]{1,0:T(8,128)(2,1)} %get-tuple-element.111.refs_4_), channel_id=1, source_target_pairs={{0,4},{1,5},{2,6},{3,7},{4,0},{5,1},{6,2},{7,3},{8,12},{9,13},{10,... | collective-permute-start | bytes 479240 | tf_op jit(solution)/shard_map/ppermute | solution.py:588
  40.5 11.0 %collective-permute-done.14.refs_6_ = bf16[96,832]{1,0:T(8,128)(2,1)S(1)} collective-permute-done((bf16[96,832]{1,0:T(8,128)(2,1)}, bf16[96,832]{1,0:T(8,128)(2,1)S(1)}, u32[]{:S(2)}, u32[]{:S(2)}) %collective-permute-start.14) | collective-permute-done | bytes 159776 | tf_op jit(solution)/shard_map/ppermute | solution.py:588
  53.1 2.5 collective-permute-start.36
  56.7 9.7 %shard_map.248 = (bf16[512,768]{1,0:T(8,128)(2,1)}, bf16[3,512,64]{2,1,0:T(8,128)(2,1)}, bf16[3,512,64]{2,1,0:T(8,128)(2,1)}, bf16[3,512,64]{2,1,0:T(8,128)(2,1)...) custom-call(s32[2]{0:T(128)} %pad_add_fusion.idx_ref, ...), custom_call_target="tpu_custom_call" | custom-call | flops 2000000000 | bytes 5931016 | tf_op jit(solution)/shard_map/pallas_call | solution.py:53
  66.5 2.2 collective-permute-start.12
  70.2 2.5 shard_map.252
  78.1 3.5 %collective-permute-done.11.refs_2_.refs_8_ = bf16[512,192]{1,0:T(8,128)(2,1)S(1)} collective-permute-done((bf16[512,192]{1,0:T(8,128)(2,1)}, bf16[512,192]{1,0:T(8,128)(2,1)S(1)}, u32[]{:S(2)}, u32[]{:S(2)}) %collective-permute-start.11) | collective-permute-done | bytes 196640 | tf_op jit(solution)/shard_map/ppermute | solution.py:588
  83.0 3.7 %shard_map.249 = (f32[128,768]{1,0:T(8,128)}, bf16[768,768]{1,0:T(8,128)(2,1)}, bf16[768,64]{1,0:T(8,128)(2,1)}, bf16[48,768]{1,0:T(8,128)(2,1)}, bf16[48,768]{1...) custom-call(s32[2]{0:T(128)} %pad_add_fusion.idx_ref, ...), custom_call_target="tpu_custom_call" | custom-call | flops 100000000 | bytes 4547592 | tf_op jit(solution)/shard_map/pallas_call | solution.py:53
  89.2 2.0 collective-permute-start.24
  95.0 3.0 collective-permute-done.23.refs_4_
  99.5 2.3 collective-permute-start.26
  102.7 2.6 collective-permute-done.26.refs_7_
  106.0 2.4 shard_map.250
  108.3 2.6 collective-permute-start.48
  115.0 14.4 %collective-permute-done.53.refs_10_ = bf16[192,384]{1,0:T(8,128)(2,1)S(1)} collective-permute-done((bf16[192,384]{1,0:T(8,128)(2,1)S(1)}, bf16[192,384]{1,0:T(8,128)(2,1)S(1)}, u32[]{:S(2)}, u32[]{:S(2)}) %collective-permute-start.53) | collective-permute-done | bytes 147488 | tf_op jit(solution)/shard_map/ppermute | solution.py:588
  135.3 12.1 %shard_map.254 = (bf16[192,768]{1,0:T(8,128)(2,1)}, bf16[192,768]{1,0:T(8,128)(2,1)}, bf16[192,768]{1,0:T(8,128)(2,1)}, bf16[192,768]{1,0:T(8,128)(2,1)}, bf16[1...) custom-call(s32[2]{0:T(128)} %pad_add_fusion.idx_ref, ...), custom_call_target="tpu_custom_call" | custom-call | flops 3623878656 | bytes 9437184 | tf_op jit(solution)/shard_map/pallas_call | solution.py:382
  152.5 12.1 %shard_map.253 = (bf16[192,768]{1,0:T(8,128)(2,1)}, bf16[192,768]{1,0:T(8,128)(2,1)}, bf16[192,768]{1,0:T(8,128)(2,1)}, bf16[192,768]{1,0:T(8,128)(2,1)}, bf16[1...) custom-call(s32[2]{0:T(128)} %pad_add_fusion.idx_ref, ...), custom_call_target="tpu_custom_call" | custom-call | flops 3623878656 | bytes 9437184 | tf_op jit(solution)/shard_map/pallas_call | solution.py:382
  168.2 6.6 %collective-permute-done.58.refs_1_ = bf16[192,768]{1,0:T(8,128)(2,1)S(1)} collective-permute-done((bf16[192,768]{1,0:T(8,128)(2,1)}, bf16[192,768]{1,0:T(8,128)(2,1)S(1)}, u32[]{:S(2)}, u32[]{:S(2)}) %collective-permute-start.58) | collective-permute-done | bytes 294944 | tf_op jit(solution)/shard_map/ppermute | solution.py:588
  174.7 4.0 %collective-permute-done.59.refs_2_ = bf16[192,768]{1,0:T(8,128)(2,1)S(1)} collective-permute-done((bf16[192,768]{1,0:T(8,128)(2,1)}, bf16[192,768]{1,0:T(8,128)(2,1)S(1)}, u32[]{:S(2)}, u32[]{:S(2)}) %collective-permute-start.59) | collective-permute-done | bytes 294944 | tf_op jit(solution)/shard_map/ppermute | solution.py:588
  179.5 3.0 %shard_map.257 = (bf16[48,768]{1,0:T(8,128)(2,1)}, bf16[48,768]{1,0:T(8,128)(2,1)}, bf16[48,768]{1,0:T(8,128)(2,1)}, bf16[48,768]{1,0:T(8,128)(2,1)}, bf16[48,76...) custom-call(s32[2]{0:T(128)} %pad_add_fusion.idx_ref, ...), custom_call_target="tpu_custom_call" | custom-call | flops 100000000 | bytes 2953736 | tf_op jit(solution)/shard_map/pallas_call | solution.py:53
  189.8 2.0 collective-permute-start.70
  191.8 5.4 %collective-permute-done.67.refs_4_ = bf16[48,768]{1,0:T(8,128)(2,1)S(1)} collective-permute-done((bf16[48,768]{1,0:T(8,128)(2,1)}, bf16[48,768]{1,0:T(8,128)(2,1)S(1)}, u32[]{:S(2)}, u32[]{:S(2)}) %collective-permute-start.67) | collective-permute-done | bytes 73760 | tf_op jit(solution)/shard_map/ppermute | solution.py:588
  199.1 3.2 %shard_map.258 = (f32[128,768]{1,0:T(8,128)}, bf16[128,768]{1,0:T(8,128)(2,1)}, f32[8,768]{1,0:T(8,128)}) custom-call(s32[2]{0:T(128)} %pad_add_fusion.idx_ref, s32[128,2]{1,0:T(8,128)} %bitcast.20, f32[128,768]{1,0:T(8,128)} %get-tuple-element.112.mixed_ref, f32[8,768]{1,0:T(8,128)} %get-tuple-element.109.gain_ref, bf16[128,768]{1,0:T(8,128)(2,1)} %bitcast.31, ...), custom_call_target="tpu_custom_call" | custom-call | flops 100000000 | bytes 1819656 | tf_op jit(solution)/shard_map/pallas_call | solution.py:53
  208.3 2.9 collective-permute-done.73.refs_5_
  212.2 3.3 %collective-permute-done.72.refs_4_ = bf16[128,768]{1,0:T(8,128)(2,1)S(1)} collective-permute-done((bf16[128,768]{1,0:T(8,128)(2,1)}, bf16[128,768]{1,0:T(8,128)(2,1)S(1)}, u32[]{:S(2)}, u32[]{:S(2)}) %collective-permute-start.72) | collective-permute-done | bytes 196640 | tf_op jit(solution)/shard_map/ppermute | solution.py:588
  218.6 11.6 %shard_map.259 = (bf16[384,896]{1,0:T(8,128)(2,1)}, bf16[384,896]{1,0:T(8,128)(2,1)}, bf16[128,768]{1,0:T(8,128)(2,1)}, bf16[128,768]{1,0:T(8,128)(2,1)}, bf16[1...) custom-call(s32[2]{0:T(128)} %pad_add_fusion.idx_ref, bf16[512,768]{1,0:T(8,128)(2,1)} %get-tuple-element.161.x_ref, ...), custom_call_target="tpu_custom_call" | custom-call | flops 4000000000 | bytes 9691144 | tf_op jit(solution)/shard_map/pallas_call | solution.py:53
  230.4 9.5 %collective-permute-done.44.refs_2_ = bf16[192,768]{1,0:T(8,128)(2,1)S(1)} collective-permute-done((bf16[192,768]{1,0:T(8,128)(2,1)S(1)}, bf16[192,768]{1,0:T(8,128)(2,1)S(1)}, u32[]{:S(2)}, u32[]{:S(2)}) %collective-permute-start.44) | collective-permute-done | bytes 294944 | tf_op jit(solution)/shard_map/ppermute | solution.py:588
  240.7 3.1 %shard_map.255 = bf16[384,768]{1,0:T(8,128)(2,1)} custom-call(s32[2]{0:T(128)} %pad_add_fusion.idx_ref, s32[3,384]{1,0:T(4,128)} %constant.13.clone.order_ref, bf16[192,768]{1,0:T(8,128)(2,1)} %get-tuple-element.133.refs_0_, bf16[192,768]{1,0:T(8,128)(2,1)} %copy-done.11, bf16[192,768]{1,0:T(8,128)(2,1)} %copy-done.12, bf16[192,768]{1,0:T(8,128)(2,1)} %copy-done.13, ...), custom_call_target="tpu_custom_call" | custom-call | flops 100000000 | bytes 2953736 | tf_op jit(solution)/shard_map/pallas_call | solution.py:53
  243.8 5.4 %all-to-all-start = ((bf16[8,48,768]{2,1,0:T(8,128)(2,1)}), bf16[8,48,768]{2,1,0:T(8,128)(2,1)S(1)}, u32[]{:S(2)}, u32[]{:S(2)}) async-start(bf16[8,48,768]{2,1,0:T(8,128)(2,1)} %bitcast.17), calls=%async_computation | async-start | bytes 1179648 | tf_op jit(solution)/shard_map/all_to_all | solution.py:681
  250.0 2.2 shard_map.261
  252.2 2.1 collective-permute-start.78
  255.3 2.3 collective-permute-start.79
  258.8 5.0 %collective-permute-done.78.refs_1_ = bf16[96,896]{1,0:T(8,128)(2,1)S(1)} collective-permute-done((bf16[96,896]{1,0:T(8,128)(2,1)}, bf16[96,896]{1,0:T(8,128)(2,1)S(1)}, u32[]{:S(2)}, u32[]{:S(2)}) %collective-permute-start.78) | collective-permute-done | bytes 172064 | tf_op jit(solution)/shard_map/ppermute | solution.py:588
  265.3 8.8 %shard_map.264 = (f32[8,768,768]{2,1,0:T(8,128)}, f32[8,768,768]{2,1,0:T(8,128)}) custom-call(bf16[4,192,768]{2,1,0:T(8,128)(2,1)} %get-tuple-element.196.rows_ref, bf16[4,192,768]{2,1,0:T(8,128)(2,1)} %get-tuple-element.197.up_ref, bf16[4,192,768]{2,1,0:T(8,128)(2,1)} %get-tuple-element.198.act_ref, bf16[4,192,768]{2,1,0:T(8,128)(2,1)} %get-tuple-element.199.pre_ref), custom_call_target="tpu_custom_call" | custom-call | flops 1811939328 | bytes 18874368 | tf_op jit(solution)/shard_map/pallas_call | solution.py:405
  274.1 3.4 %collective-permute-done.79.refs_2_ = bf16[96,896]{1,0:T(8,128)(2,1)S(1)} collective-permute-done((bf16[96,896]{1,0:T(8,128)(2,1)}, bf16[96,896]{1,0:T(8,128)(2,1)S(1)}, u32[]{:S(2)}, u32[]{:S(2)}) %collective-permute-start.79) | collective-permute-done | bytes 172064 | tf_op jit(solution)/shard_map/ppermute | solution.py:588
  283.7 8.8 %shard_map.265 = (f32[8,768,768]{2,1,0:T(8,128)}, f32[8,768,768]{2,1,0:T(8,128)}) custom-call(bf16[4,192,768]{2,1,0:T(8,128)(2,1)} %get-tuple-element.192.rows_ref, bf16[4,192,768]{2,1,0:T(8,128)(2,1)} %get-tuple-element.193.up_ref, bf16[4,192,768]{2,1,0:T(8,128)(2,1)} %get-tuple-element.194.act_ref, ...), custom_call_target="tpu_custom_call", output_to_operand_aliasing={{0}: (4, {}), {1}: (5, {})} | custom-call | flops 1811939328 | bytes 18874368 | tf_op jit(solution)/shard_map/pallas_call | solution.py:405
  293.3 2.4 shard_map.260
  296.5 2.6 shard_map.256
  300.6 2.6 shard_map.263
  (335 shorter events, 78.4 us)
Async XLA Ops:
  10.6 22.3 %collective-permute-start.3 = (bf16[96,640]{1,0:T(8,128)(2,1)}, bf16[96,640]{1,0:T(8,128)(2,1)S(1)}, u32[]{:S(2)}, u32[]{:S(2)}) collective-permute-start(bf16[96,640]{1,0:T(8,128)(2,1)} %get-tuple-element.108.refs_0_), channel_id=1, source_target_pairs={{0,1},{1,0},{2,3},{3,2},{4,5},{5,4},{6,7},{7,6},{8,9},{9,8},{10,11... | collective-permute-start | bytes 368648 | tf_op jit(solution)/shard_map/ppermute | solution.py:588
  10.8 14.7 %collective-permute-start.33 = (bf16[48,896]{1,0:T(8,128)(2,1)}, bf16[48,896]{1,0:T(8,128)(2,1)S(1)}, u32[]{:S(2)}, u32[]{:S(2)}) collective-permute-start(bf16[48,896]{1,0:T(8,128)(2,1)} %get-tuple-element.126), channel_id=1, source_target_pairs={{0,4},{1,5},{2,6},{3,7},{4,0},{5,1},{6,2},{7,3},{8,12},{9,13},{10,... | collective-permute-start | bytes 258056 | tf_op jit(solution)/shard_map/ppermute | solution.py:588
  13.8 21.7 %collective-permute-start.2 = (bf16[96,640]{1,0:T(8,128)(2,1)}, bf16[96,640]{1,0:T(8,128)(2,1)S(1)}, u32[]{:S(2)}, u32[]{:S(2)}) collective-permute-start(bf16[96,640]{1,0:T(8,128)(2,1)} %get-tuple-element.108.refs_0_), channel_id=1, source_target_pairs={{0,6},{1,7},{2,4},{3,5},{4,2},{5,3},{6,0},{7,1},{8,14},{9,15},{10,... | collective-permute-start | bytes 368648 | tf_op jit(solution)/shard_map/ppermute | solution.py:588
  17.2 13.3 %collective-permute-start.35 = (bf16[48,896]{1,0:T(8,128)(2,1)}, bf16[48,896]{1,0:T(8,128)(2,1)S(1)}, u32[]{:S(2)}, u32[]{:S(2)}) collective-permute-start(bf16[48,896]{1,0:T(8,128)(2,1)} %get-tuple-element.128), channel_id=1, source_target_pairs={{0,6},{1,7},{2,4},{3,5},{4,2},{5,3},{6,0},{7,1},{8,14},{9,15},{10,... | collective-permute-start | bytes 258056 | tf_op jit(solution)/shard_map/ppermute | solution.py:588
  25.5 13.7 %collective-permute-start.1 = (bf16[96,640]{1,0:T(8,128)(2,1)}, bf16[96,640]{1,0:T(8,128)(2,1)S(1)}, u32[]{:S(2)}, u32[]{:S(2)}) collective-permute-start(bf16[96,640]{1,0:T(8,128)(2,1)} %get-tuple-element.108.refs_0_), channel_id=1, source_target_pairs={{0,4},{1,5},{2,6},{3,7},{4,0},{5,1},{6,2},{7,3},{8,12},{9,13},{10,... | collective-permute-start | bytes 368648 | tf_op jit(solution)/shard_map/ppermute | solution.py:588
  26.3 13.4 %collective-permute-start = (bf16[96,640]{1,0:T(8,128)(2,1)}, bf16[96,640]{1,0:T(8,128)(2,1)S(1)}, u32[]{:S(2)}, u32[]{:S(2)}) collective-permute-start(bf16[96,640]{1,0:T(8,128)(2,1)} %get-tuple-element.108.refs_0_), channel_id=1, source_target_pairs={{0,2},{1,3},{2,0},{3,1},{4,6},{5,7},{6,4},{7,5},{8,10},{9,11},{10,... | collective-permute-start | bytes 368648 | tf_op jit(solution)/shard_map/ppermute | solution.py:588
  30.5 21.0 %collective-permute-start.9 = (bf16[128,768]{1,0:T(8,128)(2,1)}, bf16[128,768]{1,0:T(8,128)(2,1)S(1)}, u32[]{:S(2)}, u32[]{:S(2)}) collective-permute-start(bf16[128,768]{1,0:T(8,128)(2,1)} %bitcast.22), channel_id=1, source_target_pairs={{0,24},{8,16},{16,8},{24,0},{1,25},{9,17},{17,9},{25,1},{2,26},{10... | collective-permute-start | bytes 589832 | tf_op jit(solution)/shard_map/ppermute | solution.py:588
  35.5 16.0 %collective-permute-start.14 = (bf16[96,832]{1,0:T(8,128)(2,1)}, bf16[96,832]{1,0:T(8,128)(2,1)S(1)}, u32[]{:S(2)}, u32[]{:S(2)}) collective-permute-start(bf16[96,832]{1,0:T(8,128)(2,1)} %get-tuple-element.111.refs_4_), channel_id=1, source_target_pairs={{0,4},{1,5},{2,6},{3,7},{4,0},{5,1},{6,2},{7,3},{8,12},{9,13},{10,... | collective-permute-start | bytes 479240 | tf_op jit(solution)/shard_map/ppermute | solution.py:588
  52.0 16.9 %collective-permute-start.16 = (bf16[96,832]{1,0:T(8,128)(2,1)}, bf16[96,832]{1,0:T(8,128)(2,1)S(1)}, u32[]{:S(2)}, u32[]{:S(2)}) collective-permute-start(bf16[96,832]{1,0:T(8,128)(2,1)} %get-tuple-element.111.refs_4_), channel_id=1, source_target_pairs={{0,1},{1,0},{2,3},{3,2},{4,5},{5,4},{6,7},{7,6},{8,9},{9,8},{10,11... | collective-permute-start | bytes 479240 | tf_op jit(solution)/shard_map/ppermute | solution.py:588
  52.1 16.6 %collective-permute-start.13 = (bf16[96,832]{1,0:T(8,128)(2,1)}, bf16[96,832]{1,0:T(8,128)(2,1)S(1)}, u32[]{:S(2)}, u32[]{:S(2)}) collective-permute-start(bf16[96,832]{1,0:T(8,128)(2,1)} %get-tuple-element.111.refs_4_), channel_id=1, source_target_pairs={{0,2},{1,3},{2,0},{3,1},{4,6},{5,7},{6,4},{7,5},{8,10},{9,11},{10,... | collective-permute-start | bytes 479240 | tf_op jit(solution)/shard_map/ppermute | solution.py:588
  53.1 13.4 %collective-permute-start.36 = (bf16[48,896]{1,0:T(8,128)(2,1)}, bf16[48,896]{1,0:T(8,128)(2,1)S(1)}, u32[]{:S(2)}, u32[]{:S(2)}) collective-permute-start(bf16[48,896]{1,0:T(8,128)(2,1)} %get-tuple-element.129), channel_id=1, source_target_pairs={{0,7},{1,6},{2,5},{3,4},{4,3},{5,2},{6,1},{7,0},{8,15},{9,14},{10,... | collective-permute-start | bytes 258056 | tf_op jit(solution)/shard_map/ppermute | solution.py:588
  55.6 14.0 %collective-permute-start.19 = (bf16[96,832]{1,0:T(8,128)(2,1)S(1)}, bf16[96,832]{1,0:T(8,128)(2,1)S(1)}, u32[]{:S(2)}, u32[]{:S(2)}) collective-permute-start(bf16[96,832]{1,0:T(8,128)(2,1)S(1)} %collective-permute-done.15.refs_7_), channel_id=1, source_target_pairs={{0,1},{1,0},{2,3},{3,2},{4,5},{5,4},{6,7},{7,6},{8,9},{9,8},{10,11... | collective-permute-start | bytes 479240 | tf_op jit(solution)/shard_map/ppermute | solution.py:588
  56.0 16.6 %collective-permute-start.18 = (bf16[96,832]{1,0:T(8,128)(2,1)S(1)}, bf16[96,832]{1,0:T(8,128)(2,1)S(1)}, u32[]{:S(2)}, u32[]{:S(2)}) collective-permute-start(bf16[96,832]{1,0:T(8,128)(2,1)S(1)} %collective-permute-done.14.refs_6_), channel_id=1, source_target_pairs={{0,1},{1,0},{2,3},{3,2},{4,5},{5,4},{6,7},{7,6},{8,9},{9,8},{10,11... | collective-permute-start | bytes 479240 | tf_op jit(solution)/shard_map/ppermute | solution.py:588
  68.9 12.8 %collective-permute-start.11 = (bf16[512,192]{1,0:T(8,128)(2,1)}, bf16[512,192]{1,0:T(8,128)(2,1)S(1)}, u32[]{:S(2)}, u32[]{:S(2)}) collective-permute-start(bf16[512,192]{1,0:T(8,128)(2,1)} %get-tuple-element.110.refs_0_.refs_6_), channel_id=1, source_target_pairs={{0,16},{8,24},{16,0},{24,8},{1,17},{9,25},{17,1},{25,9},{2,18},{10... | collective-permute-start | bytes 589832 | tf_op jit(solution)/shard_map/ppermute | solution.py:588
  72.6 15.3 %collective-permute-start.39 = (bf16[192,384]{1,0:T(8,128)(2,1)}, bf16[192,384]{1,0:T(8,128)(2,1)S(1)}, u32[]{:S(2)}, u32[]{:S(2)}) collective-permute-start(bf16[192,384]{1,0:T(8,128)(2,1)} %get-tuple-element.130.refs_4_), channel_id=1, source_target_pairs={{0,16},{8,24},{16,0},{24,8},{1,17},{9,25},{17,1},{25,9},{2,18},{10... | collective-permute-start | bytes 442376 | tf_op jit(solution)/shard_map/ppermute | solution.py:588
  74.0 14.7 %collective-permute-start.37 = (bf16[192,384]{1,0:T(8,128)(2,1)}, bf16[192,384]{1,0:T(8,128)(2,1)S(1)}, u32[]{:S(2)}, u32[]{:S(2)}) collective-permute-start(bf16[192,384]{1,0:T(8,128)(2,1)} %get-tuple-element.130.refs_4_), channel_id=1, source_target_pairs={{0,8},{8,0},{16,24},{24,16},{1,9},{9,1},{17,25},{25,17},{2,10},{10... | collective-permute-start | bytes 442376 | tf_op jit(solution)/shard_map/ppermute | solution.py:588
  91.3 19.7 %collective-permute-start.40 = (bf16[192,512]{1,0:T(8,128)(2,1)S(1)}, bf16[192,512]{1,0:T(8,128)(2,1)S(1)}, u32[]{:S(2)}, u32[]{:S(2)}) collective-permute-start(bf16[192,512]{1,0:T(8,128)(2,1)S(1)} %copy-done.23), channel_id=1, source_target_pairs={{0,16},{8,24},{16,0},{24,8},{1,17},{9,25},{17,1},{25,9},{2,18},{10... | collective-permute-start | bytes 589832 | tf_op jit(solution)/shard_map/ppermute | solution.py:588
  92.3 18.9 %collective-permute-start.38 = (bf16[192,512]{1,0:T(8,128)(2,1)S(1)}, bf16[192,512]{1,0:T(8,128)(2,1)S(1)}, u32[]{:S(2)}, u32[]{:S(2)}) collective-permute-start(bf16[192,512]{1,0:T(8,128)(2,1)S(1)} %copy-done.23), channel_id=1, source_target_pairs={{0,8},{8,0},{16,24},{24,16},{1,9},{9,1},{17,25},{25,17},{2,10},{10... | collective-permute-start | bytes 589832 | tf_op jit(solution)/shard_map/ppermute | solution.py:588
  108.3 23.4 %collective-permute-start.48 = (bf16[192,768]{1,0:T(8,128)(2,1)}, bf16[192,768]{1,0:T(8,128)(2,1)S(1)}, u32[]{:S(2)}, u32[]{:S(2)}) collective-permute-start(bf16[192,768]{1,0:T(8,128)(2,1)} %get-tuple-element.137.refs_0_), channel_id=1, source_target_pairs={{0,24},{8,16},{16,8},{24,0},{1,25},{9,17},{17,9},{25,1},{2,26},{10... | collective-permute-start | bytes 884744 | tf_op jit(solution)/shard_map/ppermute | solution.py:588
  111.0 22.1 %collective-permute-start.47 = (bf16[192,768]{1,0:T(8,128)(2,1)}, bf16[192,768]{1,0:T(8,128)(2,1)S(1)}, u32[]{:S(2)}, u32[]{:S(2)}) collective-permute-start(bf16[192,768]{1,0:T(8,128)(2,1)} %get-tuple-element.137.refs_0_), channel_id=1, source_target_pairs={{0,16},{8,24},{16,0},{24,8},{1,17},{9,25},{17,1},{25,9},{2,18},{10... | collective-permute-start | bytes 884744 | tf_op jit(solution)/shard_map/ppermute | solution.py:588
  111.2 23.0 %collective-permute-start.46 = (bf16[192,768]{1,0:T(8,128)(2,1)}, bf16[192,768]{1,0:T(8,128)(2,1)S(1)}, u32[]{:S(2)}, u32[]{:S(2)}) collective-permute-start(bf16[192,768]{1,0:T(8,128)(2,1)} %get-tuple-element.137.refs_0_), channel_id=1, source_target_pairs={{0,8},{8,0},{16,24},{24,16},{1,9},{9,1},{17,25},{25,17},{2,10},{10... | collective-permute-start | bytes 884744 | tf_op jit(solution)/shard_map/ppermute | solution.py:588
  112.5 18.1 %collective-permute-start.54 = (bf16[192,512]{1,0:T(8,128)(2,1)S(1)}, bf16[192,512]{1,0:T(8,128)(2,1)S(1)}, u32[]{:S(2)}, u32[]{:S(2)}) collective-permute-start(bf16[192,512]{1,0:T(8,128)(2,1)S(1)} %collective-permute-done.52.refs_9_), channel_id=1, source_target_pairs={{0,8},{8,0},{16,24},{24,16},{1,9},{9,1},{17,25},{25,17},{2,10},{10... | collective-permute-start | bytes 589832 | tf_op jit(solution)/shard_map/ppermute | solution.py:588
  113.3 16.2 %collective-permute-start.53 = (bf16[192,384]{1,0:T(8,128)(2,1)S(1)}, bf16[192,384]{1,0:T(8,128)(2,1)S(1)}, u32[]{:S(2)}, u32[]{:S(2)}) collective-permute-start(bf16[192,384]{1,0:T(8,128)(2,1)S(1)} %collective-permute-done.49.refs_6_), channel_id=1, source_target_pairs={{0,16},{8,24},{16,0},{24,8},{1,17},{9,25},{17,1},{25,9},{2,18},{10... | collective-permute-start | bytes 442376 | tf_op jit(solution)/shard_map/ppermute | solution.py:588
  129.5 18.0 %collective-permute-start.41 = (bf16[192,384]{1,0:T(8,128)(2,1)S(1)}, bf16[192,384]{1,0:T(8,128)(2,1)S(1)}, u32[]{:S(2)}, u32[]{:S(2)}) collective-permute-start(bf16[192,384]{1,0:T(8,128)(2,1)S(1)} %collective-permute-done.37.refs_6_), channel_id=1, source_target_pairs={{0,16},{8,24},{16,0},{24,8},{1,17},{9,25},{17,1},{25,9},{2,18},{10... | collective-permute-start | bytes 442376 | tf_op jit(solution)/shard_map/ppermute | solution.py:588
  130.6 17.9 %collective-permute-start.42 = (bf16[192,512]{1,0:T(8,128)(2,1)S(1)}, bf16[192,512]{1,0:T(8,128)(2,1)S(1)}, u32[]{:S(2)}, u32[]{:S(2)}) collective-permute-start(bf16[192,512]{1,0:T(8,128)(2,1)S(1)} %collective-permute-done.40.refs_9_), channel_id=1, source_target_pairs={{0,8},{8,0},{16,24},{24,16},{1,9},{9,1},{17,25},{25,17},{2,10},{10... | collective-permute-start | bytes 589832 | tf_op jit(solution)/shard_map/ppermute | solution.py:588
  131.7 17.9 %collective-permute-start.29 = (bf16[192,768]{1,0:T(8,128)(2,1)}, bf16[192,768]{1,0:T(8,128)(2,1)S(1)}, u32[]{:S(2)}, u32[]{:S(2)}) collective-permute-start(bf16[192,768]{1,0:T(8,128)(2,1)} %get-tuple-element.121.refs_0_), channel_id=1, source_target_pairs={{0,24},{8,16},{16,8},{24,0},{1,25},{9,17},{17,9},{25,1},{2,26},{10... | collective-permute-start | bytes 884744 | tf_op jit(solution)/shard_map/ppermute | solution.py:588
  133.1 18.0 %collective-permute-start.28 = (bf16[192,768]{1,0:T(8,128)(2,1)}, bf16[192,768]{1,0:T(8,128)(2,1)S(1)}, u32[]{:S(2)}, u32[]{:S(2)}) collective-permute-start(bf16[192,768]{1,0:T(8,128)(2,1)} %get-tuple-element.121.refs_0_), channel_id=1, source_target_pairs={{0,16},{8,24},{16,0},{24,8},{1,17},{9,25},{17,1},{25,9},{2,18},{10... | collective-permute-start | bytes 884744 | tf_op jit(solution)/shard_map/ppermute | solution.py:588
  134.2 16.8 %collective-permute-start.27 = (bf16[192,768]{1,0:T(8,128)(2,1)}, bf16[192,768]{1,0:T(8,128)(2,1)S(1)}, u32[]{:S(2)}, u32[]{:S(2)}) collective-permute-start(bf16[192,768]{1,0:T(8,128)(2,1)} %get-tuple-element.121.refs_0_), channel_id=1, source_target_pairs={{0,8},{8,0},{16,24},{24,16},{1,9},{9,1},{17,25},{25,17},{2,10},{10... | collective-permute-start | bytes 884744 | tf_op jit(solution)/shard_map/ppermute | solution.py:588
  147.5 19.2 %collective-permute-start.61 = (bf16[192,768]{1,0:T(8,128)(2,1)}, bf16[192,768]{1,0:T(8,128)(2,1)S(1)}, u32[]{:S(2)}, u32[]{:S(2)}) collective-permute-start(bf16[192,768]{1,0:T(8,128)(2,1)} %get-tuple-element.149), channel_id=1, source_target_pairs={{0,8},{8,0},{16,24},{24,16},{1,9},{9,1},{17,25},{25,17},{2,10},{10... | collective-permute-start | bytes 884744 | tf_op jit(solution)/shard_map/ppermute | solution.py:588
  148.5 19.6 %collective-permute-start.62 = (bf16[192,768]{1,0:T(8,128)(2,1)}, bf16[192,768]{1,0:T(8,128)(2,1)S(1)}, u32[]{:S(2)}, u32[]{:S(2)}) collective-permute-start(bf16[192,768]{1,0:T(8,128)(2,1)} %get-tuple-element.150), channel_id=1, source_target_pairs={{0,16},{8,24},{16,0},{24,8},{1,17},{9,25},{17,1},{25,9},{2,18},{10... | collective-permute-start | bytes 884744 | tf_op jit(solution)/shard_map/ppermute | solution.py:588
  149.6 18.6 %collective-permute-start.63 = (bf16[192,768]{1,0:T(8,128)(2,1)}, bf16[192,768]{1,0:T(8,128)(2,1)S(1)}, u32[]{:S(2)}, u32[]{:S(2)}) collective-permute-start(bf16[192,768]{1,0:T(8,128)(2,1)} %get-tuple-element.151), channel_id=1, source_target_pairs={{0,24},{8,16},{16,8},{24,0},{1,25},{9,17},{17,9},{25,1},{2,26},{10... | collective-permute-start | bytes 884744 | tf_op jit(solution)/shard_map/ppermute | solution.py:588
  165.6 13.1 %collective-permute-start.59 = (bf16[192,768]{1,0:T(8,128)(2,1)}, bf16[192,768]{1,0:T(8,128)(2,1)S(1)}, u32[]{:S(2)}, u32[]{:S(2)}) collective-permute-start(bf16[192,768]{1,0:T(8,128)(2,1)} %get-tuple-element.146), channel_id=1, source_target_pairs={{0,16},{8,24},{16,0},{24,8},{1,17},{9,25},{17,1},{25,9},{2,18},{10... | collective-permute-start | bytes 884744 | tf_op jit(solution)/shard_map/ppermute | solution.py:588
  184.5 22.5 %collective-permute-start.55 = (bf16[192,768]{1,0:T(8,128)(2,1)S(1)}, bf16[192,768]{1,0:T(8,128)(2,1)S(1)}, u32[]{:S(2)}, u32[]{:S(2)}) collective-permute-start(bf16[192,768]{1,0:T(8,128)(2,1)S(1)} %copy-done.79), channel_id=1, source_target_pairs={{0,8},{8,0},{16,24},{24,16},{1,9},{9,1},{17,25},{25,17},{2,10},{10... | collective-permute-start | bytes 884744 | tf_op jit(solution)/shard_map/ppermute | solution.py:588
  205.8 24.5 %collective-permute-start.56 = (bf16[192,768]{1,0:T(8,128)(2,1)S(1)}, bf16[192,768]{1,0:T(8,128)(2,1)S(1)}, u32[]{:S(2)}, u32[]{:S(2)}) collective-permute-start(bf16[192,768]{1,0:T(8,128)(2,1)S(1)} %copy-done.76), channel_id=1, source_target_pairs={{0,16},{8,24},{16,0},{24,8},{1,17},{9,25},{17,1},{25,9},{2,18},{10... | collective-permute-start | bytes 884744 | tf_op jit(solution)/shard_map/ppermute | solution.py:588
  207.0 23.4 %collective-permute-start.57 = (bf16[192,768]{1,0:T(8,128)(2,1)S(1)}, bf16[192,768]{1,0:T(8,128)(2,1)S(1)}, u32[]{:S(2)}, u32[]{:S(2)}) collective-permute-start(bf16[192,768]{1,0:T(8,128)(2,1)S(1)} %copy-done.75), channel_id=1, source_target_pairs={{0,24},{8,16},{16,8},{24,0},{1,25},{9,17},{17,9},{25,1},{2,26},{10... | collective-permute-start | bytes 884744 | tf_op jit(solution)/shard_map/ppermute | solution.py:588
  211.2 19.1 %collective-permute-start.43 = (bf16[192,768]{1,0:T(8,128)(2,1)}, bf16[192,768]{1,0:T(8,128)(2,1)S(1)}, u32[]{:S(2)}, u32[]{:S(2)}) collective-permute-start(bf16[192,768]{1,0:T(8,128)(2,1)} %get-tuple-element.134), channel_id=1, source_target_pairs={{0,8},{8,0},{16,24},{24,16},{1,9},{9,1},{17,25},{25,17},{2,10},{10... | collective-permute-start | bytes 884744 | tf_op jit(solution)/shard_map/ppermute | solution.py:588
  215.5 24.4 %collective-permute-start.44 = (bf16[192,768]{1,0:T(8,128)(2,1)S(1)}, bf16[192,768]{1,0:T(8,128)(2,1)S(1)}, u32[]{:S(2)}, u32[]{:S(2)}) collective-permute-start(bf16[192,768]{1,0:T(8,128)(2,1)S(1)} %copy-done.78), channel_id=1, source_target_pairs={{0,16},{8,24},{16,0},{24,8},{1,17},{9,25},{17,1},{25,9},{2,18},{10... | collective-permute-start | bytes 884744 | tf_op jit(solution)/shard_map/ppermute | solution.py:588
  217.3 22.6 %collective-permute-start.45 = (bf16[192,768]{1,0:T(8,128)(2,1)S(1)}, bf16[192,768]{1,0:T(8,128)(2,1)S(1)}, u32[]{:S(2)}, u32[]{:S(2)}) collective-permute-start(bf16[192,768]{1,0:T(8,128)(2,1)S(1)} %copy-done.77), channel_id=1, source_target_pairs={{0,24},{8,16},{16,8},{24,0},{1,25},{9,17},{17,9},{25,1},{2,26},{10... | collective-permute-start | bytes 884744 | tf_op jit(solution)/shard_map/ppermute | solution.py:588
  230.3 18.9 %collective-permute-start.77 = (bf16[384,896]{1,0:T(8,128)(2,1)}, bf16[384,896]{1,0:T(8,128)(2,1)S(1)}, u32[]{:S(2)}, u32[]{:S(2)}) collective-permute-start(bf16[384,896]{1,0:T(8,128)(2,1)} %get-tuple-element.179), channel_id=1, source_target_pairs={{0,1},{1,0},{2,3},{3,2},{4,5},{5,4},{6,7},{7,6},{8,9},{9,8},{10,11... | collective-permute-start | bytes 2064392 | tf_op jit(solution)/shard_map/ppermute | solution.py:588
  243.8 51.9 %all-to-all-start = ((bf16[8,48,768]{2,1,0:T(8,128)(2,1)}), bf16[8,48,768]{2,1,0:T(8,128)(2,1)S(1)}, u32[]{:S(2)}, u32[]{:S(2)}) async-start(bf16[8,48,768]{2,1,0:T(8,128)(2,1)} %bitcast.17), calls=%async_computation | async-start | bytes 1179648 | tf_op jit(solution)/shard_map/all_to_all | solution.py:681
  254.3 28.3 %collective-permute-start.74 = (bf16[128,768]{1,0:T(8,128)(2,1)S(1)}, bf16[128,768]{1,0:T(8,128)(2,1)S(1)}, u32[]{:S(2)}, u32[]{:S(2)}) collective-permute-start(bf16[128,768]{1,0:T(8,128)(2,1)S(1)} %copy-done.82), channel_id=1, source_target_pairs={{0,8},{8,0},{16,24},{24,16},{1,9},{9,1},{17,25},{25,17},{2,10},{10... | collective-permute-start | bytes 589832 | tf_op jit(solution)/shard_map/ppermute | solution.py:588
  255.3 22.3 %collective-permute-start.79 = (bf16[96,896]{1,0:T(8,128)(2,1)}, bf16[96,896]{1,0:T(8,128)(2,1)S(1)}, u32[]{:S(2)}, u32[]{:S(2)}) collective-permute-start(bf16[96,896]{1,0:T(8,128)(2,1)} %get-tuple-element.182), channel_id=1, source_target_pairs={{0,4},{1,5},{2,6},{3,7},{4,0},{5,1},{6,2},{7,3},{8,12},{9,13},{10,... | collective-permute-start | bytes 516104 | tf_op jit(solution)/shard_map/ppermute | solution.py:588
  257.6 20.0 %collective-permute-start.80 = (bf16[96,896]{1,0:T(8,128)(2,1)}, bf16[96,896]{1,0:T(8,128)(2,1)S(1)}, u32[]{:S(2)}, u32[]{:S(2)}) collective-permute-start(bf16[96,896]{1,0:T(8,128)(2,1)} %get-tuple-element.183), channel_id=1, source_target_pairs={{0,6},{1,7},{2,4},{3,5},{4,2},{5,3},{6,0},{7,1},{8,14},{9,15},{10,... | collective-permute-start | bytes 516104 | tf_op jit(solution)/shard_map/ppermute | solution.py:588
  257.7 34.8 %collective-permute-start.75 = (bf16[128,768]{1,0:T(8,128)(2,1)S(1)}, bf16[128,768]{1,0:T(8,128)(2,1)S(1)}, u32[]{:S(2)}, u32[]{:S(2)}) collective-permute-start(bf16[128,768]{1,0:T(8,128)(2,1)S(1)} %copy-done.81), channel_id=1, source_target_pairs={{0,16},{8,24},{16,0},{24,8},{1,17},{9,25},{17,1},{25,9},{2,18},{10... | collective-permute-start | bytes 589832 | tf_op jit(solution)/shard_map/ppermute | solution.py:588
  263.8 28.8 %collective-permute-start.76 = (bf16[128,768]{1,0:T(8,128)(2,1)S(1)}, bf16[128,768]{1,0:T(8,128)(2,1)S(1)}, u32[]{:S(2)}, u32[]{:S(2)}) collective-permute-start(bf16[128,768]{1,0:T(8,128)(2,1)S(1)} %copy-done.80), channel_id=1, source_target_pairs={{0,24},{8,16},{16,8},{24,0},{1,25},{9,17},{17,9},{25,1},{2,26},{10... | collective-permute-start | bytes 589832 | tf_op jit(solution)/shard_map/ppermute | solution.py:588
  280.2 18.9 %collective-permute-start.83 = (bf16[96,896]{1,0:T(8,128)(2,1)}, bf16[96,896]{1,0:T(8,128)(2,1)S(1)}, u32[]{:S(2)}, u32[]{:S(2)}) collective-permute-start(bf16[96,896]{1,0:T(8,128)(2,1)} %shard_map.262.refs_0_), channel_id=1, source_target_pairs={{0,24},{8,16},{16,8},{24,0},{1,25},{9,17},{17,9},{25,1},{2,26},{10... | collective-permute-start | bytes 516104 | tf_op jit(solution)/shard_map/ppermute | solution.py:588
  281.8 17.4 %collective-permute-start.82 = (bf16[96,896]{1,0:T(8,128)(2,1)}, bf16[96,896]{1,0:T(8,128)(2,1)S(1)}, u32[]{:S(2)}, u32[]{:S(2)}) collective-permute-start(bf16[96,896]{1,0:T(8,128)(2,1)} %shard_map.262.refs_0_), channel_id=1, source_target_pairs={{0,16},{8,24},{16,0},{24,8},{1,17},{9,25},{17,1},{25,9},{2,18},{10... | collective-permute-start | bytes 516104 | tf_op jit(solution)/shard_map/ppermute | solution.py:588
  282.6 16.5 %collective-permute-start.81 = (bf16[96,896]{1,0:T(8,128)(2,1)}, bf16[96,896]{1,0:T(8,128)(2,1)S(1)}, u32[]{:S(2)}, u32[]{:S(2)}) collective-permute-start(bf16[96,896]{1,0:T(8,128)(2,1)} %shard_map.262.refs_0_), channel_id=1, source_target_pairs={{0,8},{8,0},{16,24},{24,16},{1,9},{9,1},{17,25},{25,17},{2,10},{10... | collective-permute-start | bytes 516104 | tf_op jit(solution)/shard_map/ppermute | solution.py:588
  (133 other events, 1527.1 us)

commit v2 on v1

--- a/solution.py
+++ b/solution.py
@@ -592,6 +592,14 @@
     return [first] + [permute(x, axis, k, n) for k, x in zip(range(1, n), rest, strict=True)]
 
 
+def spread_far_first(first, rest, n):
+    got = [first] + [None] * (n - 1)
+    for ks in (range(n // 2, n), range(1, n // 2)):
+        for k in ks:
+            got[k] = permute(rest[k - 1], "ep", k, n)
+    return got
+
+
 def two_steps(parts):
     got = []
     for part, (near, via) in zip(parts, ((1, 2), (2, 1)), strict=True):
@@ -654,7 +662,7 @@
     orders = jnp.asarray(np.stack([to, to - source * CAP, source]), jnp.int32)
 
     def to_experts(sent, cuts):
-        got = spread(sent[0], sent[1:], "ep", NE)
+        got = spread_far_first(sent[0], sent[1:], NE)
         parts = call(
             functools.partial(arrange, cfg, cuts), [order, *got],
             [((E * CAP // HALVES, hi - lo), bf) for lo, hi in cuts] * HALVES, n_smem=0,
@@ -679,7 +687,7 @@
         )
         if whole:
             return [lax.all_to_all(sent[0], "ep", split_axis=0, concat_axis=0, tiled=True)]
-        return spread(sent[0], sent[1:], "ep", NE)
+        return spread_far_first(sent[0], sent[1:], NE)
 
     W2 = D + EXTRA
     cut = (D // 2 + EXTRA - 1) // EXTRA * EXTRA

time: 305 us -> 305 us (level)
  no operation moved by 1% of the time
where the time goes in v2:
time: 305 us; the launch traced here: 303 us
  starting transfers between devices  105 us (34%)
  Pallas kernels  97.4 us (32%)
  waiting for transfers between devices  87.1 us (29%)
  local copies, waits for them, and re-layouts  11.6 us (4%)
    ppermute x84, starting transfers between devices, permute(): return lax.ppermute(x, axis, [(i, i ^ k) for i in range(n)])  99.6 us
    ppermute x84, waiting for transfers between devices, permute(): return lax.ppermute(x, axis, [(i, i ^ k) for i in range(n)])  87.1 us
    pallas_call x15, Pallas kernels, call(): pl.pallas_call(kernel, out_shape=[jax.ShapeDtypeStruct(s, d) for s, d in...  55.6 us
    pallas_call x2, Pallas kernels, experts(): pl.pallas_call(functools.partial(expert_kernel, cfg, first, len(cuts)), g...  24.2 us
    pallas_call x2, Pallas kernels, expert_weights(): pl.pallas_call(expert_weights_kernel, grid=(steps,), out_shape=[jax.Shape...  17.6 us
    unnamed x193, local copies, waits for them, and re-layouts  11.6 us
  transfers between devices with their start and end apart: 85, of which 20 were waited for; matrix products, arithmetic and copies ran while one was open for 0% of the time, Pallas kernels for 29%

profile of v2, /device:TPU:0, one launch (start us, length us, event | category | flops | bytes accessed | tf_op | source)
XLA Modules:
  0.0 303.2 jit_solution(10579409942098020232)
XLA Ops:
  2.7 2.5 shard_map.251
  5.7 2.6 collective-permute-start.31
  8.4 2.2 shard_map.247
  10.8 3.0 collective-permute-start.33
  13.8 3.4 %collective-permute-start.2 = (bf16[96,640]{1,0:T(8,128)(2,1)}, bf16[96,640]{1,0:T(8,128)(2,1)S(1)}, u32[]{:S(2)}, u32[]{:S(2)}) collective-permute-start(bf16[96,640]{1,0:T(8,128)(2,1)} %get-tuple-element.108.refs_0_), channel_id=1, source_target_pairs={{0,6},{1,7},{2,4},{3,5},{4,2},{5,3},{6,0},{7,1},{8,14},{9,15},{10,... | collective-permute-start | bytes 368648 | tf_op jit(solution)/shard_map/ppermute | solution.py:588
  17.6 7.8 %collective-permute-done.33.refs_4_ = bf16[48,896]{1,0:T(8,128)(2,1)S(1)} collective-permute-done((bf16[48,896]{1,0:T(8,128)(2,1)}, bf16[48,896]{1,0:T(8,128)(2,1)S(1)}, u32[]{:S(2)}, u32[]{:S(2)}) %collective-permute-start.33) | collective-permute-done | bytes 86048 | tf_op jit(solution)/shard_map/ppermute | solution.py:588
  26.3 4.2 %collective-permute-start = (bf16[96,640]{1,0:T(8,128)(2,1)}, bf16[96,640]{1,0:T(8,128)(2,1)S(1)}, u32[]{:S(2)}, u32[]{:S(2)}) collective-permute-start(bf16[96,640]{1,0:T(8,128)(2,1)} %get-tuple-element.108.refs_0_), channel_id=1, source_target_pairs={{0,2},{1,3},{2,0},{3,1},{4,6},{5,7},{6,4},{7,5},{8,10},{9,11},{10,... | collective-permute-start | bytes 368648 | tf_op jit(solution)/shard_map/ppermute | solution.py:588
  30.5 2.4 collective-permute-start.9
  32.9 2.5 collective-permute-start.15
  35.5 3.7 %collective-permute-start.14 = (bf16[96,832]{1,0:T(8,128)(2,1)}, bf16[96,832]{1,0:T(8,128)(2,1)S(1)}, u32[]{:S(2)}, u32[]{:S(2)}) collective-permute-start(bf16[96,832]{1,0:T(8,128)(2,1)} %get-tuple-element.111.refs_4_), channel_id=1, source_target_pairs={{0,4},{1,5},{2,6},{3,7},{4,0},{5,1},{6,2},{7,3},{8,12},{9,13},{10,... | collective-permute-start | bytes 479240 | tf_op jit(solution)/shard_map/ppermute | solution.py:588
  40.5 11.0 %collective-permute-done.14.refs_6_ = bf16[96,832]{1,0:T(8,128)(2,1)S(1)} collective-permute-done((bf16[96,832]{1,0:T(8,128)(2,1)}, bf16[96,832]{1,0:T(8,128)(2,1)S(1)}, u32[]{:S(2)}, u32[]{:S(2)}) %collective-permute-start.14) | collective-permute-done | bytes 159776 | tf_op jit(solution)/shard_map/ppermute | solution.py:588
  53.1 2.5 collective-permute-start.36
  56.7 9.7 %shard_map.248 = (bf16[512,768]{1,0:T(8,128)(2,1)}, bf16[3,512,64]{2,1,0:T(8,128)(2,1)}, bf16[3,512,64]{2,1,0:T(8,128)(2,1)}, bf16[3,512,64]{2,1,0:T(8,128)(2,1)...) custom-call(s32[2]{0:T(128)} %pad_add_fusion.idx_ref, ...), custom_call_target="tpu_custom_call" | custom-call | flops 2000000000 | bytes 5931016 | tf_op jit(solution)/shard_map/pallas_call | solution.py:53
  66.5 2.2 collective-permute-start.12
  70.2 2.5 shard_map.252
  78.1 3.5 %collective-permute-done.11.refs_2_.refs_8_ = bf16[512,192]{1,0:T(8,128)(2,1)S(1)} collective-permute-done((bf16[512,192]{1,0:T(8,128)(2,1)}, bf16[512,192]{1,0:T(8,128)(2,1)S(1)}, u32[]{:S(2)}, u32[]{:S(2)}) %collective-permute-start.11) | collective-permute-done | bytes 196640 | tf_op jit(solution)/shard_map/ppermute | solution.py:588
  83.0 3.7 %shard_map.249 = (f32[128,768]{1,0:T(8,128)}, bf16[768,768]{1,0:T(8,128)(2,1)}, bf16[768,64]{1,0:T(8,128)(2,1)}, bf16[48,768]{1,0:T(8,128)(2,1)}, bf16[48,768]{1...) custom-call(s32[2]{0:T(128)} %pad_add_fusion.idx_ref, ...), custom_call_target="tpu_custom_call" | custom-call | flops 100000000 | bytes 4547592 | tf_op jit(solution)/shard_map/pallas_call | solution.py:53
  89.2 2.0 collective-permute-start.24
  95.0 3.0 collective-permute-done.23.refs_4_
  99.5 2.3 collective-permute-start.26
  102.7 2.6 collective-permute-done.26.refs_7_
  106.0 2.4 shard_map.250
  108.3 2.6 collective-permute-start.48
  115.0 14.4 %collective-permute-done.53.refs_10_ = bf16[192,384]{1,0:T(8,128)(2,1)S(1)} collective-permute-done((bf16[192,384]{1,0:T(8,128)(2,1)S(1)}, bf16[192,384]{1,0:T(8,128)(2,1)S(1)}, u32[]{:S(2)}, u32[]{:S(2)}) %collective-permute-start.53) | collective-permute-done | bytes 147488 | tf_op jit(solution)/shard_map/ppermute | solution.py:588
  135.3 12.1 %shard_map.254 = (bf16[192,768]{1,0:T(8,128)(2,1)}, bf16[192,768]{1,0:T(8,128)(2,1)}, bf16[192,768]{1,0:T(8,128)(2,1)}, bf16[192,768]{1,0:T(8,128)(2,1)}, bf16[1...) custom-call(s32[2]{0:T(128)} %pad_add_fusion.idx_ref, ...), custom_call_target="tpu_custom_call" | custom-call | flops 3623878656 | bytes 9437184 | tf_op jit(solution)/shard_map/pallas_call | solution.py:382
  152.5 12.1 %shard_map.253 = (bf16[192,768]{1,0:T(8,128)(2,1)}, bf16[192,768]{1,0:T(8,128)(2,1)}, bf16[192,768]{1,0:T(8,128)(2,1)}, bf16[192,768]{1,0:T(8,128)(2,1)}, bf16[1...) custom-call(s32[2]{0:T(128)} %pad_add_fusion.idx_ref, ...), custom_call_target="tpu_custom_call" | custom-call | flops 3623878656 | bytes 9437184 | tf_op jit(solution)/shard_map/pallas_call | solution.py:382
  168.2 6.6 %collective-permute-done.58.refs_1_ = bf16[192,768]{1,0:T(8,128)(2,1)S(1)} collective-permute-done((bf16[192,768]{1,0:T(8,128)(2,1)}, bf16[192,768]{1,0:T(8,128)(2,1)S(1)}, u32[]{:S(2)}, u32[]{:S(2)}) %collective-permute-start.58) | collective-permute-done | bytes 294944 | tf_op jit(solution)/shard_map/ppermute | solution.py:588
  174.7 4.0 %collective-permute-done.59.refs_2_ = bf16[192,768]{1,0:T(8,128)(2,1)S(1)} collective-permute-done((bf16[192,768]{1,0:T(8,128)(2,1)}, bf16[192,768]{1,0:T(8,128)(2,1)S(1)}, u32[]{:S(2)}, u32[]{:S(2)}) %collective-permute-start.59) | collective-permute-done | bytes 294944 | tf_op jit(solution)/shard_map/ppermute | solution.py:588
  179.5 3.0 %shard_map.257 = (bf16[48,768]{1,0:T(8,128)(2,1)}, bf16[48,768]{1,0:T(8,128)(2,1)}, bf16[48,768]{1,0:T(8,128)(2,1)}, bf16[48,768]{1,0:T(8,128)(2,1)}, bf16[48,76...) custom-call(s32[2]{0:T(128)} %pad_add_fusion.idx_ref, ...), custom_call_target="tpu_custom_call" | custom-call | flops 100000000 | bytes 2953736 | tf_op jit(solution)/shard_map/pallas_call | solution.py:53
  189.8 2.0 collective-permute-start.70
  191.8 5.4 %collective-permute-done.67.refs_4_ = bf16[48,768]{1,0:T(8,128)(2,1)S(1)} collective-permute-done((bf16[48,768]{1,0:T(8,128)(2,1)}, bf16[48,768]{1,0:T(8,128)(2,1)S(1)}, u32[]{:S(2)}, u32[]{:S(2)}) %collective-permute-start.67) | collective-permute-done | bytes 73760 | tf_op jit(solution)/shard_map/ppermute | solution.py:588
  199.1 3.2 %shard_map.258 = (f32[128,768]{1,0:T(8,128)}, bf16[128,768]{1,0:T(8,128)(2,1)}, f32[8,768]{1,0:T(8,128)}) custom-call(s32[2]{0:T(128)} %pad_add_fusion.idx_ref, s32[128,2]{1,0:T(8,128)} %bitcast.20, f32[128,768]{1,0:T(8,128)} %get-tuple-element.112.mixed_ref, f32[8,768]{1,0:T(8,128)} %get-tuple-element.109.gain_ref, bf16[128,768]{1,0:T(8,128)(2,1)} %bitcast.31, ...), custom_call_target="tpu_custom_call" | custom-call | flops 100000000 | bytes 1819656 | tf_op jit(solution)/shard_map/pallas_call | solution.py:53
  208.3 2.9 collective-permute-done.73.refs_5_
  212.2 3.3 %collective-permute-done.72.refs_4_ = bf16[128,768]{1,0:T(8,128)(2,1)S(1)} collective-permute-done((bf16[128,768]{1,0:T(8,128)(2,1)}, bf16[128,768]{1,0:T(8,128)(2,1)S(1)}, u32[]{:S(2)}, u32[]{:S(2)}) %collective-permute-start.72) | collective-permute-done | bytes 196640 | tf_op jit(solution)/shard_map/ppermute | solution.py:588
  218.6 11.6 %shard_map.259 = (bf16[384,896]{1,0:T(8,128)(2,1)}, bf16[384,896]{1,0:T(8,128)(2,1)}, bf16[128,768]{1,0:T(8,128)(2,1)}, bf16[128,768]{1,0:T(8,128)(2,1)}, bf16[1...) custom-call(s32[2]{0:T(128)} %pad_add_fusion.idx_ref, bf16[512,768]{1,0:T(8,128)(2,1)} %get-tuple-element.161.x_ref, ...), custom_call_target="tpu_custom_call" | custom-call | flops 4000000000 | bytes 9691144 | tf_op jit(solution)/shard_map/pallas_call | solution.py:53
  230.4 9.5 %collective-permute-done.44.refs_2_ = bf16[192,768]{1,0:T(8,128)(2,1)S(1)} collective-permute-done((bf16[192,768]{1,0:T(8,128)(2,1)S(1)}, bf16[192,768]{1,0:T(8,128)(2,1)S(1)}, u32[]{:S(2)}, u32[]{:S(2)}) %collective-permute-start.44) | collective-permute-done | bytes 294944 | tf_op jit(solution)/shard_map/ppermute | solution.py:588
  240.7 3.1 %shard_map.255 = bf16[384,768]{1,0:T(8,128)(2,1)} custom-call(s32[2]{0:T(128)} %pad_add_fusion.idx_ref, s32[3,384]{1,0:T(4,128)} %constant.13.clone.order_ref, bf16[192,768]{1,0:T(8,128)(2,1)} %get-tuple-element.133.refs_0_, bf16[192,768]{1,0:T(8,128)(2,1)} %copy-done.11, bf16[192,768]{1,0:T(8,128)(2,1)} %copy-done.12, bf16[192,768]{1,0:T(8,128)(2,1)} %copy-done.13, ...), custom_call_target="tpu_custom_call" | custom-call | flops 100000000 | bytes 2953736 | tf_op jit(solution)/shard_map/pallas_call | solution.py:53
  243.8 5.4 %all-to-all-start = ((bf16[8,48,768]{2,1,0:T(8,128)(2,1)}), bf16[8,48,768]{2,1,0:T(8,128)(2,1)S(1)}, u32[]{:S(2)}, u32[]{:S(2)}) async-start(bf16[8,48,768]{2,1,0:T(8,128)(2,1)} %bitcast.17), calls=%async_computation | async-start | bytes 1179648 | tf_op jit(solution)/shard_map/all_to_all | solution.py:689
  250.0 2.2 shard_map.261
  252.2 2.1 collective-permute-start.78
  255.3 2.3 collective-permute-start.79
  258.8 5.0 %collective-permute-done.78.refs_1_ = bf16[96,896]{1,0:T(8,128)(2,1)S(1)} collective-permute-done((bf16[96,896]{1,0:T(8,128)(2,1)}, bf16[96,896]{1,0:T(8,128)(2,1)S(1)}, u32[]{:S(2)}, u32[]{:S(2)}) %collective-permute-start.78) | collective-permute-done | bytes 172064 | tf_op jit(solution)/shard_map/ppermute | solution.py:588
  265.3 8.8 %shard_map.264 = (f32[8,768,768]{2,1,0:T(8,128)}, f32[8,768,768]{2,1,0:T(8,128)}) custom-call(bf16[4,192,768]{2,1,0:T(8,128)(2,1)} %get-tuple-element.196.rows_ref, bf16[4,192,768]{2,1,0:T(8,128)(2,1)} %get-tuple-element.197.up_ref, bf16[4,192,768]{2,1,0:T(8,128)(2,1)} %get-tuple-element.198.act_ref, bf16[4,192,768]{2,1,0:T(8,128)(2,1)} %get-tuple-element.199.pre_ref), custom_call_target="tpu_custom_call" | custom-call | flops 1811939328 | bytes 18874368 | tf_op jit(solution)/shard_map/pallas_call | solution.py:405
  274.1 3.4 %collective-permute-done.79.refs_2_ = bf16[96,896]{1,0:T(8,128)(2,1)S(1)} collective-permute-done((bf16[96,896]{1,0:T(8,128)(2,1)}, bf16[96,896]{1,0:T(8,128)(2,1)S(1)}, u32[]{:S(2)}, u32[]{:S(2)}) %collective-permute-start.79) | collective-permute-done | bytes 172064 | tf_op jit(solution)/shard_map/ppermute | solution.py:588
  283.7 8.8 %shard_map.265 = (f32[8,768,768]{2,1,0:T(8,128)}, f32[8,768,768]{2,1,0:T(8,128)}) custom-call(bf16[4,192,768]{2,1,0:T(8,128)(2,1)} %get-tuple-element.192.rows_ref, bf16[4,192,768]{2,1,0:T(8,128)(2,1)} %get-tuple-element.193.up_ref, bf16[4,192,768]{2,1,0:T(8,128)(2,1)} %get-tuple-element.194.act_ref, ...), custom_call_target="tpu_custom_call", output_to_operand_aliasing={{0}: (4, {}), {1}: (5, {})} | custom-call | flops 1811939328 | bytes 18874368 | tf_op jit(solution)/shard_map/pallas_call | solution.py:405
  293.3 2.4 shard_map.260
  296.5 2.6 shard_map.256
  300.6 2.6 shard_map.263
  (335 shorter events, 78.4 us)
Async XLA Ops:
  10.6 22.3 %collective-permute-start.3 = (bf16[96,640]{1,0:T(8,128)(2,1)}, bf16[96,640]{1,0:T(8,128)(2,1)S(1)}, u32[]{:S(2)}, u32[]{:S(2)}) collective-permute-start(bf16[96,640]{1,0:T(8,128)(2,1)} %get-tuple-element.108.refs_0_), channel_id=1, source_target_pairs={{0,1},{1,0},{2,3},{3,2},{4,5},{5,4},{6,7},{7,6},{8,9},{9,8},{10,11... | collective-permute-start | bytes 368648 | tf_op jit(solution)/shard_map/ppermute | solution.py:588
  10.8 14.7 %collective-permute-start.33 = (bf16[48,896]{1,0:T(8,128)(2,1)}, bf16[48,896]{1,0:T(8,128)(2,1)S(1)}, u32[]{:S(2)}, u32[]{:S(2)}) collective-permute-start(bf16[48,896]{1,0:T(8,128)(2,1)} %get-tuple-element.126), channel_id=1, source_target_pairs={{0,4},{1,5},{2,6},{3,7},{4,0},{5,1},{6,2},{7,3},{8,12},{9,13},{10,... | collective-permute-start | bytes 258056 | tf_op jit(solution)/shard_map/ppermute | solution.py:588
  13.8 21.7 %collective-permute-start.2 = (bf16[96,640]{1,0:T(8,128)(2,1)}, bf16[96,640]{1,0:T(8,128)(2,1)S(1)}, u32[]{:S(2)}, u32[]{:S(2)}) collective-permute-start(bf16[96,640]{1,0:T(8,128)(2,1)} %get-tuple-element.108.refs_0_), channel_id=1, source_target_pairs={{0,6},{1,7},{2,4},{3,5},{4,2},{5,3},{6,0},{7,1},{8,14},{9,15},{10,... | collective-permute-start | bytes 368648 | tf_op jit(solution)/shard_map/ppermute | solution.py:588
  17.2 13.3 %collective-permute-start.35 = (bf16[48,896]{1,0:T(8,128)(2,1)}, bf16[48,896]{1,0:T(8,128)(2,1)S(1)}, u32[]{:S(2)}, u32[]{:S(2)}) collective-permute-start(bf16[48,896]{1,0:T(8,128)(2,1)} %get-tuple-element.128), channel_id=1, source_target_pairs={{0,6},{1,7},{2,4},{3,5},{4,2},{5,3},{6,0},{7,1},{8,14},{9,15},{10,... | collective-permute-start | bytes 258056 | tf_op jit(solution)/shard_map/ppermute | solution.py:588
  25.5 13.7 %collective-permute-start.1 = (bf16[96,640]{1,0:T(8,128)(2,1)}, bf16[96,640]{1,0:T(8,128)(2,1)S(1)}, u32[]{:S(2)}, u32[]{:S(2)}) collective-permute-start(bf16[96,640]{1,0:T(8,128)(2,1)} %get-tuple-element.108.refs_0_), channel_id=1, source_target_pairs={{0,4},{1,5},{2,6},{3,7},{4,0},{5,1},{6,2},{7,3},{8,12},{9,13},{10,... | collective-permute-start | bytes 368648 | tf_op jit(solution)/shard_map/ppermute | solution.py:588
  26.3 13.4 %collective-permute-start = (bf16[96,640]{1,0:T(8,128)(2,1)}, bf16[96,640]{1,0:T(8,128)(2,1)S(1)}, u32[]{:S(2)}, u32[]{:S(2)}) collective-permute-start(bf16[96,640]{1,0:T(8,128)(2,1)} %get-tuple-element.108.refs_0_), channel_id=1, source_target_pairs={{0,2},{1,3},{2,0},{3,1},{4,6},{5,7},{6,4},{7,5},{8,10},{9,11},{10,... | collective-permute-start | bytes 368648 | tf_op jit(solution)/shard_map/ppermute | solution.py:588
  30.5 21.0 %collective-permute-start.9 = (bf16[128,768]{1,0:T(8,128)(2,1)}, bf16[128,768]{1,0:T(8,128)(2,1)S(1)}, u32[]{:S(2)}, u32[]{:S(2)}) collective-permute-start(bf16[128,768]{1,0:T(8,128)(2,1)} %bitcast.22), channel_id=1, source_target_pairs={{0,24},{8,16},{16,8},{24,0},{1,25},{9,17},{17,9},{25,1},{2,26},{10... | collective-permute-start | bytes 589832 | tf_op jit(solution)/shard_map/ppermute | solution.py:588
  35.5 16.0 %collective-permute-start.14 = (bf16[96,832]{1,0:T(8,128)(2,1)}, bf16[96,832]{1,0:T(8,128)(2,1)S(1)}, u32[]{:S(2)}, u32[]{:S(2)}) collective-permute-start(bf16[96,832]{1,0:T(8,128)(2,1)} %get-tuple-element.111.refs_4_), channel_id=1, source_target_pairs={{0,4},{1,5},{2,6},{3,7},{4,0},{5,1},{6,2},{7,3},{8,12},{9,13},{10,... | collective-permute-start | bytes 479240 | tf_op jit(solution)/shard_map/ppermute | solution.py:588
  52.0 16.9 %collective-permute-start.16 = (bf16[96,832]{1,0:T(8,128)(2,1)}, bf16[96,832]{1,0:T(8,128)(2,1)S(1)}, u32[]{:S(2)}, u32[]{:S(2)}) collective-permute-start(bf16[96,832]{1,0:T(8,128)(2,1)} %get-tuple-element.111.refs_4_), channel_id=1, source_target_pairs={{0,1},{1,0},{2,3},{3,2},{4,5},{5,4},{6,7},{7,6},{8,9},{9,8},{10,11... | collective-permute-start | bytes 479240 | tf_op jit(solution)/shard_map/ppermute | solution.py:588
  52.1 16.6 %collective-permute-start.13 = (bf16[96,832]{1,0:T(8,128)(2,1)}, bf16[96,832]{1,0:T(8,128)(2,1)S(1)}, u32[]{:S(2)}, u32[]{:S(2)}) collective-permute-start(bf16[96,832]{1,0:T(8,128)(2,1)} %get-tuple-element.111.refs_4_), channel_id=1, source_target_pairs={{0,2},{1,3},{2,0},{3,1},{4,6},{5,7},{6,4},{7,5},{8,10},{9,11},{10,... | collective-permute-start | bytes 479240 | tf_op jit(solution)/shard_map/ppermute | solution.py:588
  53.1 13.4 %collective-permute-start.36 = (bf16[48,896]{1,0:T(8,128)(2,1)}, bf16[48,896]{1,0:T(8,128)(2,1)S(1)}, u32[]{:S(2)}, u32[]{:S(2)}) collective-permute-start(bf16[48,896]{1,0:T(8,128)(2,1)} %get-tuple-element.129), channel_id=1, source_target_pairs={{0,7},{1,6},{2,5},{3,4},{4,3},{5,2},{6,1},{7,0},{8,15},{9,14},{10,... | collective-permute-start | bytes 258056 | tf_op jit(solution)/shard_map/ppermute | solution.py:588
  55.6 14.0 %collective-permute-start.19 = (bf16[96,832]{1,0:T(8,128)(2,1)S(1)}, bf16[96,832]{1,0:T(8,128)(2,1)S(1)}, u32[]{:S(2)}, u32[]{:S(2)}) collective-permute-start(bf16[96,832]{1,0:T(8,128)(2,1)S(1)} %collective-permute-done.15.refs_7_), channel_id=1, source_target_pairs={{0,1},{1,0},{2,3},{3,2},{4,5},{5,4},{6,7},{7,6},{8,9},{9,8},{10,11... | collective-permute-start | bytes 479240 | tf_op jit(solution)/shard_map/ppermute | solution.py:588
  56.0 16.6 %collective-permute-start.18 = (bf16[96,832]{1,0:T(8,128)(2,1)S(1)}, bf16[96,832]{1,0:T(8,128)(2,1)S(1)}, u32[]{:S(2)}, u32[]{:S(2)}) collective-permute-start(bf16[96,832]{1,0:T(8,128)(2,1)S(1)} %collective-permute-done.14.refs_6_), channel_id=1, source_target_pairs={{0,1},{1,0},{2,3},{3,2},{4,5},{5,4},{6,7},{7,6},{8,9},{9,8},{10,11... | collective-permute-start | bytes 479240 | tf_op jit(solution)/shard_map/ppermute | solution.py:588
  68.9 12.8 %collective-permute-start.11 = (bf16[512,192]{1,0:T(8,128)(2,1)}, bf16[512,192]{1,0:T(8,128)(2,1)S(1)}, u32[]{:S(2)}, u32[]{:S(2)}) collective-permute-start(bf16[512,192]{1,0:T(8,128)(2,1)} %get-tuple-element.110.refs_0_.refs_6_), channel_id=1, source_target_pairs={{0,16},{8,24},{16,0},{24,8},{1,17},{9,25},{17,1},{25,9},{2,18},{10... | collective-permute-start | bytes 589832 | tf_op jit(solution)/shard_map/ppermute | solution.py:588
  72.6 15.3 %collective-permute-start.39 = (bf16[192,384]{1,0:T(8,128)(2,1)}, bf16[192,384]{1,0:T(8,128)(2,1)S(1)}, u32[]{:S(2)}, u32[]{:S(2)}) collective-permute-start(bf16[192,384]{1,0:T(8,128)(2,1)} %get-tuple-element.130.refs_4_), channel_id=1, source_target_pairs={{0,16},{8,24},{16,0},{24,8},{1,17},{9,25},{17,1},{25,9},{2,18},{10... | collective-permute-start | bytes 442376 | tf_op jit(solution)/shard_map/ppermute | solution.py:588
  74.0 14.7 %collective-permute-start.37 = (bf16[192,384]{1,0:T(8,128)(2,1)}, bf16[192,384]{1,0:T(8,128)(2,1)S(1)}, u32[]{:S(2)}, u32[]{:S(2)}) collective-permute-start(bf16[192,384]{1,0:T(8,128)(2,1)} %get-tuple-element.130.refs_4_), channel_id=1, source_target_pairs={{0,8},{8,0},{16,24},{24,16},{1,9},{9,1},{17,25},{25,17},{2,10},{10... | collective-permute-start | bytes 442376 | tf_op jit(solution)/shard_map/ppermute | solution.py:588
  91.3 19.7 %collective-permute-start.40 = (bf16[192,512]{1,0:T(8,128)(2,1)S(1)}, bf16[192,512]{1,0:T(8,128)(2,1)S(1)}, u32[]{:S(2)}, u32[]{:S(2)}) collective-permute-start(bf16[192,512]{1,0:T(8,128)(2,1)S(1)} %copy-done.23), channel_id=1, source_target_pairs={{0,16},{8,24},{16,0},{24,8},{1,17},{9,25},{17,1},{25,9},{2,18},{10... | collective-permute-start | bytes 589832 | tf_op jit(solution)/shard_map/ppermute | solution.py:588
  92.3 18.9 %collective-permute-start.38 = (bf16[192,512]{1,0:T(8,128)(2,1)S(1)}, bf16[192,512]{1,0:T(8,128)(2,1)S(1)}, u32[]{:S(2)}, u32[]{:S(2)}) collective-permute-start(bf16[192,512]{1,0:T(8,128)(2,1)S(1)} %copy-done.23), channel_id=1, source_target_pairs={{0,8},{8,0},{16,24},{24,16},{1,9},{9,1},{17,25},{25,17},{2,10},{10... | collective-permute-start | bytes 589832 | tf_op jit(solution)/shard_map/ppermute | solution.py:588
  108.3 23.4 %collective-permute-start.48 = (bf16[192,768]{1,0:T(8,128)(2,1)}, bf16[192,768]{1,0:T(8,128)(2,1)S(1)}, u32[]{:S(2)}, u32[]{:S(2)}) collective-permute-start(bf16[192,768]{1,0:T(8,128)(2,1)} %get-tuple-element.137.refs_0_), channel_id=1, source_target_pairs={{0,24},{8,16},{16,8},{24,0},{1,25},{9,17},{17,9},{25,1},{2,26},{10... | collective-permute-start | bytes 884744 | tf_op jit(solution)/shard_map/ppermute | solution.py:588
  111.0 22.1 %collective-permute-start.47 = (bf16[192,768]{1,0:T(8,128)(2,1)}, bf16[192,768]{1,0:T(8,128)(2,1)S(1)}, u32[]{:S(2)}, u32[]{:S(2)}) collective-permute-start(bf16[192,768]{1,0:T(8,128)(2,1)} %get-tuple-element.137.refs_0_), channel_id=1, source_target_pairs={{0,16},{8,24},{16,0},{24,8},{1,17},{9,25},{17,1},{25,9},{2,18},{10... | collective-permute-start | bytes 884744 | tf_op jit(solution)/shard_map/ppermute | solution.py:588
  111.2 23.0 %collective-permute-start.46 = (bf16[192,768]{1,0:T(8,128)(2,1)}, bf16[192,768]{1,0:T(8,128)(2,1)S(1)}, u32[]{:S(2)}, u32[]{:S(2)}) collective-permute-start(bf16[192,768]{1,0:T(8,128)(2,1)} %get-tuple-element.137.refs_0_), channel_id=1, source_target_pairs={{0,8},{8,0},{16,24},{24,16},{1,9},{9,1},{17,25},{25,17},{2,10},{10... | collective-permute-start | bytes 884744 | tf_op jit(solution)/shard_map/ppermute | solution.py:588
  112.5 18.1 %collective-permute-start.54 = (bf16[192,512]{1,0:T(8,128)(2,1)S(1)}, bf16[192,512]{1,0:T(8,128)(2,1)S(1)}, u32[]{:S(2)}, u32[]{:S(2)}) collective-permute-start(bf16[192,512]{1,0:T(8,128)(2,1)S(1)} %collective-permute-done.52.refs_9_), channel_id=1, source_target_pairs={{0,8},{8,0},{16,24},{24,16},{1,9},{9,1},{17,25},{25,17},{2,10},{10... | collective-permute-start | bytes 589832 | tf_op jit(solution)/shard_map/ppermute | solution.py:588
  113.3 16.2 %collective-permute-start.53 = (bf16[192,384]{1,0:T(8,128)(2,1)S(1)}, bf16[192,384]{1,0:T(8,128)(2,1)S(1)}, u32[]{:S(2)}, u32[]{:S(2)}) collective-permute-start(bf16[192,384]{1,0:T(8,128)(2,1)S(1)} %collective-permute-done.49.refs_6_), channel_id=1, source_target_pairs={{0,16},{8,24},{16,0},{24,8},{1,17},{9,25},{17,1},{25,9},{2,18},{10... | collective-permute-start | bytes 442376 | tf_op jit(solution)/shard_map/ppermute | solution.py:588
  129.5 18.0 %collective-permute-start.41 = (bf16[192,384]{1,0:T(8,128)(2,1)S(1)}, bf16[192,384]{1,0:T(8,128)(2,1)S(1)}, u32[]{:S(2)}, u32[]{:S(2)}) collective-permute-start(bf16[192,384]{1,0:T(8,128)(2,1)S(1)} %collective-permute-done.37.refs_6_), channel_id=1, source_target_pairs={{0,16},{8,24},{16,0},{24,8},{1,17},{9,25},{17,1},{25,9},{2,18},{10... | collective-permute-start | bytes 442376 | tf_op jit(solution)/shard_map/ppermute | solution.py:588
  130.6 17.9 %collective-permute-start.42 = (bf16[192,512]{1,0:T(8,128)(2,1)S(1)}, bf16[192,512]{1,0:T(8,128)(2,1)S(1)}, u32[]{:S(2)}, u32[]{:S(2)}) collective-permute-start(bf16[192,512]{1,0:T(8,128)(2,1)S(1)} %collective-permute-done.40.refs_9_), channel_id=1, source_target_pairs={{0,8},{8,0},{16,24},{24,16},{1,9},{9,1},{17,25},{25,17},{2,10},{10... | collective-permute-start | bytes 589832 | tf_op jit(solution)/shard_map/ppermute | solution.py:588
  131.7 17.9 %collective-permute-start.29 = (bf16[192,768]{1,0:T(8,128)(2,1)}, bf16[192,768]{1,0:T(8,128)(2,1)S(1)}, u32[]{:S(2)}, u32[]{:S(2)}) collective-permute-start(bf16[192,768]{1,0:T(8,128)(2,1)} %get-tuple-element.121.refs_0_), channel_id=1, source_target_pairs={{0,24},{8,16},{16,8},{24,0},{1,25},{9,17},{17,9},{25,1},{2,26},{10... | collective-permute-start | bytes 884744 | tf_op jit(solution)/shard_map/ppermute | solution.py:588
  133.1 18.0 %collective-permute-start.28 = (bf16[192,768]{1,0:T(8,128)(2,1)}, bf16[192,768]{1,0:T(8,128)(2,1)S(1)}, u32[]{:S(2)}, u32[]{:S(2)}) collective-permute-start(bf16[192,768]{1,0:T(8,128)(2,1)} %get-tuple-element.121.refs_0_), channel_id=1, source_target_pairs={{0,16},{8,24},{16,0},{24,8},{1,17},{9,25},{17,1},{25,9},{2,18},{10... | collective-permute-start | bytes 884744 | tf_op jit(solution)/shard_map/ppermute | solution.py:588
  134.2 16.8 %collective-permute-start.27 = (bf16[192,768]{1,0:T(8,128)(2,1)}, bf16[192,768]{1,0:T(8,128)(2,1)S(1)}, u32[]{:S(2)}, u32[]{:S(2)}) collective-permute-start(bf16[192,768]{1,0:T(8,128)(2,1)} %get-tuple-element.121.refs_0_), channel_id=1, source_target_pairs={{0,8},{8,0},{16,24},{24,16},{1,9},{9,1},{17,25},{25,17},{2,10},{10... | collective-permute-start | bytes 884744 | tf_op jit(solution)/shard_map/ppermute | solution.py:588
  147.5 19.2 %collective-permute-start.61 = (bf16[192,768]{1,0:T(8,128)(2,1)}, bf16[192,768]{1,0:T(8,128)(2,1)S(1)}, u32[]{:S(2)}, u32[]{:S(2)}) collective-permute-start(bf16[192,768]{1,0:T(8,128)(2,1)} %get-tuple-element.149), channel_id=1, source_target_pairs={{0,8},{8,0},{16,24},{24,16},{1,9},{9,1},{17,25},{25,17},{2,10},{10... | collective-permute-start | bytes 884744 | tf_op jit(solution)/shard_map/ppermute | solution.py:588
  148.5 19.6 %collective-permute-start.62 = (bf16[192,768]{1,0:T(8,128)(2,1)}, bf16[192,768]{1,0:T(8,128)(2,1)S(1)}, u32[]{:S(2)}, u32[]{:S(2)}) collective-permute-start(bf16[192,768]{1,0:T(8,128)(2,1)} %get-tuple-element.150), channel_id=1, source_target_pairs={{0,16},{8,24},{16,0},{24,8},{1,17},{9,25},{17,1},{25,9},{2,18},{10... | collective-permute-start | bytes 884744 | tf_op jit(solution)/shard_map/ppermute | solution.py:588
  149.6 18.6 %collective-permute-start.63 = (bf16[192,768]{1,0:T(8,128)(2,1)}, bf16[192,768]{1,0:T(8,128)(2,1)S(1)}, u32[]{:S(2)}, u32[]{:S(2)}) collective-permute-start(bf16[192,768]{1,0:T(8,128)(2,1)} %get-tuple-element.151), channel_id=1, source_target_pairs={{0,24},{8,16},{16,8},{24,0},{1,25},{9,17},{17,9},{25,1},{2,26},{10... | collective-permute-start | bytes 884744 | tf_op jit(solution)/shard_map/ppermute | solution.py:588
  165.6 13.1 %collective-permute-start.59 = (bf16[192,768]{1,0:T(8,128)(2,1)}, bf16[192,768]{1,0:T(8,128)(2,1)S(1)}, u32[]{:S(2)}, u32[]{:S(2)}) collective-permute-start(bf16[192,768]{1,0:T(8,128)(2,1)} %get-tuple-element.146), channel_id=1, source_target_pairs={{0,16},{8,24},{16,0},{24,8},{1,17},{9,25},{17,1},{25,9},{2,18},{10... | collective-permute-start | bytes 884744 | tf_op jit(solution)/shard_map/ppermute | solution.py:588
  184.5 22.5 %collective-permute-start.55 = (bf16[192,768]{1,0:T(8,128)(2,1)S(1)}, bf16[192,768]{1,0:T(8,128)(2,1)S(1)}, u32[]{:S(2)}, u32[]{:S(2)}) collective-permute-start(bf16[192,768]{1,0:T(8,128)(2,1)S(1)} %copy-done.79), channel_id=1, source_target_pairs={{0,8},{8,0},{16,24},{24,16},{1,9},{9,1},{17,25},{25,17},{2,10},{10... | collective-permute-start | bytes 884744 | tf_op jit(solution)/shard_map/ppermute | solution.py:588
  205.8 24.5 %collective-permute-start.56 = (bf16[192,768]{1,0:T(8,128)(2,1)S(1)}, bf16[192,768]{1,0:T(8,128)(2,1)S(1)}, u32[]{:S(2)}, u32[]{:S(2)}) collective-permute-start(bf16[192,768]{1,0:T(8,128)(2,1)S(1)} %copy-done.76), channel_id=1, source_target_pairs={{0,16},{8,24},{16,0},{24,8},{1,17},{9,25},{17,1},{25,9},{2,18},{10... | collective-permute-start | bytes 884744 | tf_op jit(solution)/shard_map/ppermute | solution.py:588
  207.0 23.4 %collective-permute-start.57 = (bf16[192,768]{1,0:T(8,128)(2,1)S(1)}, bf16[192,768]{1,0:T(8,128)(2,1)S(1)}, u32[]{:S(2)}, u32[]{:S(2)}) collective-permute-start(bf16[192,768]{1,0:T(8,128)(2,1)S(1)} %copy-done.75), channel_id=1, source_target_pairs={{0,24},{8,16},{16,8},{24,0},{1,25},{9,17},{17,9},{25,1},{2,26},{10... | collective-permute-start | bytes 884744 | tf_op jit(solution)/shard_map/ppermute | solution.py:588
  211.2 19.1 %collective-permute-start.43 = (bf16[192,768]{1,0:T(8,128)(2,1)}, bf16[192,768]{1,0:T(8,128)(2,1)S(1)}, u32[]{:S(2)}, u32[]{:S(2)}) collective-permute-start(bf16[192,768]{1,0:T(8,128)(2,1)} %get-tuple-element.134), channel_id=1, source_target_pairs={{0,8},{8,0},{16,24},{24,16},{1,9},{9,1},{17,25},{25,17},{2,10},{10... | collective-permute-start | bytes 884744 | tf_op jit(solution)/shard_map/ppermute | solution.py:588
  215.5 24.4 %collective-permute-start.44 = (bf16[192,768]{1,0:T(8,128)(2,1)S(1)}, bf16[192,768]{1,0:T(8,128)(2,1)S(1)}, u32[]{:S(2)}, u32[]{:S(2)}) collective-permute-start(bf16[192,768]{1,0:T(8,128)(2,1)S(1)} %copy-done.78), channel_id=1, source_target_pairs={{0,16},{8,24},{16,0},{24,8},{1,17},{9,25},{17,1},{25,9},{2,18},{10... | collective-permute-start | bytes 884744 | tf_op jit(solution)/shard_map/ppermute | solution.py:588
  217.3 22.6 %collective-permute-start.45 = (bf16[192,768]{1,0:T(8,128)(2,1)S(1)}, bf16[192,768]{1,0:T(8,128)(2,1)S(1)}, u32[]{:S(2)}, u32[]{:S(2)}) collective-permute-start(bf16[192,768]{1,0:T(8,128)(2,1)S(1)} %copy-done.77), channel_id=1, source_target_pairs={{0,24},{8,16},{16,8},{24,0},{1,25},{9,17},{17,9},{25,1},{2,26},{10... | collective-permute-start | bytes 884744 | tf_op jit(solution)/shard_map/ppermute | solution.py:588
  230.3 18.9 %collective-permute-start.77 = (bf16[384,896]{1,0:T(8,128)(2,1)}, bf16[384,896]{1,0:T(8,128)(2,1)S(1)}, u32[]{:S(2)}, u32[]{:S(2)}) collective-permute-start(bf16[384,896]{1,0:T(8,128)(2,1)} %get-tuple-element.179), channel_id=1, source_target_pairs={{0,1},{1,0},{2,3},{3,2},{4,5},{5,4},{6,7},{7,6},{8,9},{9,8},{10,11... | collective-permute-start | bytes 2064392 | tf_op jit(solution)/shard_map/ppermute | solution.py:588
  243.8 51.9 %all-to-all-start = ((bf16[8,48,768]{2,1,0:T(8,128)(2,1)}), bf16[8,48,768]{2,1,0:T(8,128)(2,1)S(1)}, u32[]{:S(2)}, u32[]{:S(2)}) async-start(bf16[8,48,768]{2,1,0:T(8,128)(2,1)} %bitcast.17), calls=%async_computation | async-start | bytes 1179648 | tf_op jit(solution)/shard_map/all_to_all | solution.py:689
  254.3 28.3 %collective-permute-start.74 = (bf16[128,768]{1,0:T(8,128)(2,1)S(1)}, bf16[128,768]{1,0:T(8,128)(2,1)S(1)}, u32[]{:S(2)}, u32[]{:S(2)}) collective-permute-start(bf16[128,768]{1,0:T(8,128)(2,1)S(1)} %copy-done.82), channel_id=1, source_target_pairs={{0,8},{8,0},{16,24},{24,16},{1,9},{9,1},{17,25},{25,17},{2,10},{10... | collective-permute-start | bytes 589832 | tf_op jit(solution)/shard_map/ppermute | solution.py:588
  255.3 22.3 %collective-permute-start.79 = (bf16[96,896]{1,0:T(8,128)(2,1)}, bf16[96,896]{1,0:T(8,128)(2,1)S(1)}, u32[]{:S(2)}, u32[]{:S(2)}) collective-permute-start(bf16[96,896]{1,0:T(8,128)(2,1)} %get-tuple-element.182), channel_id=1, source_target_pairs={{0,4},{1,5},{2,6},{3,7},{4,0},{5,1},{6,2},{7,3},{8,12},{9,13},{10,... | collective-permute-start | bytes 516104 | tf_op jit(solution)/shard_map/ppermute | solution.py:588
  257.6 20.0 %collective-permute-start.80 = (bf16[96,896]{1,0:T(8,128)(2,1)}, bf16[96,896]{1,0:T(8,128)(2,1)S(1)}, u32[]{:S(2)}, u32[]{:S(2)}) collective-permute-start(bf16[96,896]{1,0:T(8,128)(2,1)} %get-tuple-element.183), channel_id=1, source_target_pairs={{0,6},{1,7},{2,4},{3,5},{4,2},{5,3},{6,0},{7,1},{8,14},{9,15},{10,... | collective-permute-start | bytes 516104 | tf_op jit(solution)/shard_map/ppermute | solution.py:588
  257.7 34.8 %collective-permute-start.75 = (bf16[128,768]{1,0:T(8,128)(2,1)S(1)}, bf16[128,768]{1,0:T(8,128)(2,1)S(1)}, u32[]{:S(2)}, u32[]{:S(2)}) collective-permute-start(bf16[128,768]{1,0:T(8,128)(2,1)S(1)} %copy-done.81), channel_id=1, source_target_pairs={{0,16},{8,24},{16,0},{24,8},{1,17},{9,25},{17,1},{25,9},{2,18},{10... | collective-permute-start | bytes 589832 | tf_op jit(solution)/shard_map/ppermute | solution.py:588
  263.8 28.8 %collective-permute-start.76 = (bf16[128,768]{1,0:T(8,128)(2,1)S(1)}, bf16[128,768]{1,0:T(8,128)(2,1)S(1)}, u32[]{:S(2)}, u32[]{:S(2)}) collective-permute-start(bf16[128,768]{1,0:T(8,128)(2,1)S(1)} %copy-done.80), channel_id=1, source_target_pairs={{0,24},{8,16},{16,8},{24,0},{1,25},{9,17},{17,9},{25,1},{2,26},{10... | collective-permute-start | bytes 589832 | tf_op jit(solution)/shard_map/ppermute | solution.py:588
  280.2 18.9 %collective-permute-start.83 = (bf16[96,896]{1,0:T(8,128)(2,1)}, bf16[96,896]{1,0:T(8,128)(2,1)S(1)}, u32[]{:S(2)}, u32[]{:S(2)}) collective-permute-start(bf16[96,896]{1,0:T(8,128)(2,1)} %shard_map.262.refs_0_), channel_id=1, source_target_pairs={{0,24},{8,16},{16,8},{24,0},{1,25},{9,17},{17,9},{25,1},{2,26},{10... | collective-permute-start | bytes 516104 | tf_op jit(solution)/shard_map/ppermute | solution.py:588
  281.8 17.4 %collective-permute-start.82 = (bf16[96,896]{1,0:T(8,128)(2,1)}, bf16[96,896]{1,0:T(8,128)(2,1)S(1)}, u32[]{:S(2)}, u32[]{:S(2)}) collective-permute-start(bf16[96,896]{1,0:T(8,128)(2,1)} %shard_map.262.refs_0_), channel_id=1, source_target_pairs={{0,16},{8,24},{16,0},{24,8},{1,17},{9,25},{17,1},{25,9},{2,18},{10... | collective-permute-start | bytes 516104 | tf_op jit(solution)/shard_map/ppermute | solution.py:588
  282.6 16.5 %collective-permute-start.81 = (bf16[96,896]{1,0:T(8,128)(2,1)}, bf16[96,896]{1,0:T(8,128)(2,1)S(1)}, u32[]{:S(2)}, u32[]{:S(2)}) collective-permute-start(bf16[96,896]{1,0:T(8,128)(2,1)} %shard_map.262.refs_0_), channel_id=1, source_target_pairs={{0,8},{8,0},{16,24},{24,16},{1,9},{9,1},{17,25},{25,17},{2,10},{10... | collective-permute-start | bytes 516104 | tf_op jit(solution)/shard_map/ppermute | solution.py:588
  (133 other events, 1527.1 us)
